TPU v7x, 128 devices: a whole 4x4x4 slice. The times are simulated.
128 devices in a mesh: child: 4 (over y), tile: 32 (over x, z, core).
Axes of the slice: x: 4, y: 4, z: 4, core: 2. Of those that a mesh axis runs over, the one named last changes fastest.
Arguments:
- child_tiles: bfloat16 [4, 512, 512, 512], P('child', 'tile'), may hold values from -6 to 6
- panel: bfloat16 [4, 16384, 512], P('child', 'tile'), may hold values from -1 to 1
- bases: bfloat16 [4, 16384, 128], P('child', 'tile'), may hold values from -0.25 to 0.25
- tile_blocks: int32 [4, 512, 2], P('child'), may hold values from 0 to 31, as said below
- tile_dest: int32 [4, 512, 1], P('child'), may hold values from 0 to 31; in each aligned block of 16 rows (0 to 15, 16 to 31, ..., all dimensions but the last counted through in order) at most 2 rows name the same one
- tile_slot: int32 [4, 512], P('child'), may hold values from 0 to 7
- parent_tiles: bfloat16 [4, 256, 512, 512], P('child', 'tile'), may hold values from -6 to 6
- parent_blocks: int32 [4, 256, 2], P('child', 'tile'), may hold values from 0 to 31, as said below
- sketch_test: bfloat16 [16384, 128], replicated, may hold values from -0.25 to 0.25
Outputs:
- updated_tiles: bfloat16 [4, 256, 512, 512], P('child', 'tile')
- row_sketch: float32 [16384, 128], P(('child', 'tile'))
Inputs may be any that keep to these rules, and one draw needn't show every extreme that they name: `tile_blocks`: each tile's row block is not below its column block. `tile_dest`: among the tiles of one device (aligned blocks of 16 tiles of a child), at most 2 name the same owner. `parent_blocks`: each parent tile's row block is not below its column block.
All inputs are finite; a program needn't handle non-finite values.
Results may differ from a plain program's by a relative error of at most 0.0063.
Values may be sent and summed in bfloat16 or wider, within the bound.
A program may use at most 192 MiB of HBM per device.

v0:
```python
import math

import jax
import jax.numpy as jnp
from jax import lax
from jax.sharding import PartitionSpec as P

CAP = 2


def in_one_piece(arrays, axis, dim, along):
    both = jnp.concatenate(arrays, axis=along)
    out, at, finished = (lax.all_gather(both, axis, axis=dim, tiled=True), 0, [])
    for a in arrays:
        finished.append(lax.slice_in_dim(out, at, at + a.shape[along], axis=along))
        at += a.shape[along]
    return tuple(finished)


def cut_along(shard, dim, size):
    shape = shard.shape
    parts = shard.reshape(*shape[:dim], size, shape[dim] // size, *shape[dim + 1 :])
    return jnp.moveaxis(parts, dim, 0)


def sum_at_owner(shard, axis, dim):
    size = lax.axis_size(axis)
    parts = lax.all_to_all(cut_along(shard, dim, size), axis, 0, 0, tiled=True)
    return jnp.sum(parts.astype(jnp.float32), axis=0)


def shards(
    child_tiles,
    panel,
    bases,
    tile_blocks,
    tile_dest,
    tile_slot,
    parent_tiles,
    parent_blocks,
    sketch_test,
):
    owners = lax.axis_size("tile")
    myself = lax.axis_index("tile")
    tile_count = child_tiles.shape[1]
    tile_order = child_tiles.shape[2]
    rank_width = bases.shape[2]
    sketch_width = sketch_test.shape[1]
    parent_count = parent_tiles.shape[1]
    own_tiles = child_tiles[0]
    blocks_all = tile_blocks[0]
    own_blocks = lax.dynamic_slice_in_dim(blocks_all, myself * tile_count, tile_count, 0)
    row_ids = own_blocks[:, 0]
    col_ids = own_blocks[:, 1]
    whole_panel, whole_bases = in_one_piece((panel[0], bases[0]), "tile", 0, 1)
    panel_blocks = whole_panel.reshape(-1, tile_order, tile_order)
    basis_blocks = whole_bases.reshape(-1, tile_order, rank_width)
    left_basis = jnp.take(basis_blocks, row_ids, axis=0)
    right_basis = jnp.take(basis_blocks, col_ids, axis=0)
    left_proj = jnp.einsum(
        "qxr,qxy->qry",
        left_basis,
        jnp.take(panel_blocks, row_ids, axis=0),
        preferred_element_type=jnp.float32,
    ).astype(jnp.bfloat16)
    right_proj = jnp.einsum(
        "qxr,qxy->qry",
        right_basis,
        jnp.take(panel_blocks, col_ids, axis=0),
        preferred_element_type=jnp.float32,
    ).astype(jnp.bfloat16)
    half = jnp.einsum(
        "qxr,qxy->qry", left_basis, own_tiles, preferred_element_type=jnp.float32
    ).astype(jnp.bfloat16)
    encoded = jnp.einsum("qry,qys->qrs", half, right_basis, preferred_element_type=jnp.float32)
    cross = jnp.einsum("qrk,qsk->qrs", left_proj, right_proj, preferred_element_type=jnp.float32)
    cores = (encoded - cross).astype(jnp.bfloat16)
    dest_all = tile_dest[0, :, 0].reshape(owners, tile_count)
    own_dest = lax.dynamic_index_in_dim(dest_all, myself, 0, keepdims=False)
    targets = jnp.arange(owners, dtype=jnp.int32)
    slot_ids = jnp.arange(CAP, dtype=jnp.int32)
    hit_table = (own_dest[:, None] == targets[None, :]).astype(jnp.int32)
    before = jnp.cumsum(hit_table, axis=0) - hit_table
    position = jnp.sum(hit_table * before, axis=1)
    selector = (
        (own_dest[None, None, :] == targets[:, None, None])
        & (position[None, None, :] == slot_ids[None, :, None])
    ).astype(jnp.bfloat16)
    outgoing = jnp.einsum(
        "tkq,qrs->tkrs", selector, cores, preferred_element_type=jnp.float32
    ).astype(jnp.bfloat16)
    incoming = lax.all_to_all(outgoing, "tile", split_axis=0, concat_axis=0, tiled=True)
    arrive = (dest_all == myself).astype(jnp.int32)
    earlier = jnp.cumsum(arrive, axis=1) - arrive
    matched = arrive[:, None, :] * (earlier[:, None, :] == slot_ids[None, :, None]).astype(
        jnp.int32
    )
    rows_all = blocks_all[:, 0].reshape(owners, tile_count)
    cols_all = blocks_all[:, 1].reshape(owners, tile_count)
    slots_all = tile_slot[0].reshape(owners, tile_count)
    recv_rows = jnp.sum(matched * rows_all[:, None, :], axis=2).reshape(-1)
    recv_cols = jnp.sum(matched * cols_all[:, None, :], axis=2).reshape(-1)
    recv_slots = jnp.sum(matched * slots_all[:, None, :], axis=2).reshape(-1)
    recv_live = jnp.sum(matched, axis=2).reshape(-1)
    recv_slots = jnp.where(recv_live > 0, recv_slots, parent_count)
    items = owners * CAP
    group_size = math.gcd(items, 8)
    groups = items // group_size
    received = incoming.reshape(groups, group_size, rank_width, rank_width)
    left_bases = jnp.take(basis_blocks, recv_rows, axis=0).reshape(
        groups, group_size, tile_order, rank_width
    )
    right_bases = jnp.take(basis_blocks, recv_cols, axis=0).reshape(
        groups, group_size, tile_order, rank_width
    )
    slot_groups = recv_slots.reshape(groups, group_size)

    def decode(summed, pieces):
        left_group, right_group, core_group, slot_group = pieces
        left_part = jnp.einsum(
            "gxr,grs->gxs", left_group, core_group, preferred_element_type=jnp.float32
        ).astype(jnp.bfloat16)
        decoded = jnp.einsum(
            "gxs,gys->gxy", left_part, right_group, preferred_element_type=jnp.float32
        )
        return (summed + jax.ops.segment_sum(decoded, slot_group, num_segments=parent_count), None)

    summed, _ = lax.scan(
        decode,
        parent_tiles[0].astype(jnp.float32),
        (left_bases, right_bases, received, slot_groups),
    )
    updated = summed.astype(jnp.bfloat16)
    prow = parent_blocks[0, :, 0]
    pcol = parent_blocks[0, :, 1]
    test_blocks = sketch_test.reshape(-1, tile_order, sketch_width)
    block_total = test_blocks.shape[0]
    direct = jnp.einsum(
        "pxy,pyk->pxk",
        updated,
        jnp.take(test_blocks, pcol, axis=0),
        preferred_element_type=jnp.float32,
    )
    second = jnp.einsum(
        "pyx,pyk->pxk",
        updated,
        jnp.take(test_blocks, prow, axis=0),
        preferred_element_type=jnp.float32,
    )
    second = second * (prow != pcol).astype(jnp.float32)[:, None, None]
    partial_sketch = jax.ops.segment_sum(
        direct, prow, num_segments=block_total
    ) + jax.ops.segment_sum(second, pcol, num_segments=block_total)
    partial_sketch = partial_sketch.reshape(-1, sketch_width)
    by_child = sum_at_owner(partial_sketch.astype(jnp.bfloat16), "child", 0)
    row_sketch = sum_at_owner(by_child.astype(jnp.bfloat16), "tile", 0)
    return (updated[None], row_sketch)


def solution(mesh):
    return jax.shard_map(
        shards,
        mesh=mesh,
        in_specs=(
            P("child", "tile", None, None),
            P("child", "tile", None),
            P("child", "tile", None),
            P("child", None, None),
            P("child", None, None),
            P("child", None),
            P("child", "tile", None, None),
            P("child", "tile", None),
            P(),
        ),
        out_specs=(P("child", "tile", None, None), P(("child", "tile"), None)),
        check_vma=False,
    )
```

profile of v0, /device:TPU:0, one launch (start us, length us, event | category | flops | bytes accessed | tf_op | source)
XLA Modules:
  0.0 484.5 jit_solution(15886239285098464544)
XLA Ops:
  23.6 6.8 %bitcast_convert_fusion = f32[8,512,512]{2,1,0:T(8,128)} fusion(bf16[1,8,512,512]{3,2,1,0:T(8,128)(2,1)} %param.25), kind=kLoop, calls=%fused_computation.32 | loop fusion | flops 2097152 | bytes 12582912 | tf_op jit(solution)/shard_map/convert_element_type | solution.py:130
  30.4 65.4 %all-gather.2.cloned.1.call-done = bf16[16384,640]{1,0:T(8,128)(2,1)} async-done(((bf16[512,640]{1,0:T(8,128)(2,1)}), bf16[16384,640]{1,0:T(8,128)(2,1)}) %all-gather.2.cloned.1.call-update) | async-done | bytes 20971536 | tf_op jit(solution)/shard_map/all_gather | solution.py:13
  102.7 13.8 %slice.50 = bf16[16384,512]{1,0:T(8,128)(2,1)} slice(bf16[16384,640]{1,0:T(8,128)(2,1)} %all-gather.2.cloned.1.call-done), slice={[0:16384], [0:512]} | slice | bytes 33554432 | tf_op jit(solution)/shard_map/slice | solution.py:15
  116.5 10.4 %gather_fusion.4 = bf16[16,512,512]{2,1,0:T(8,128)(2,1)} fusion(bf16[32,512,512]{2,1,0:T(8,128)(2,1)} %bitcast.82, s32[1024]{0:T(1024)S(1)} %get-tuple-element.76), kind=kCustom, calls=%fused_computation.6.clone | custom fusion | bytes 16777280 | tf_op jit(solution)/shard_map/jit(_take)/gather | solution.py:69
  131.3 10.5 %gather_fusion.3 = bf16[16,512,512]{2,1,0:T(8,128)(2,1)} fusion(bf16[32,512,512]{2,1,0:T(8,128)(2,1)} %bitcast.83, s32[1024]{0:T(1024)S(1)} %get-tuple-element.77), kind=kCustom, calls=%fused_computation.2.clone | custom fusion | bytes 16777280 | tf_op jit(solution)/shard_map/jit(_take)/gather | solution.py:63
  141.8 6.6 %fusion.16 = bf16[16,128,512]{2,1,0:T(8,128)(2,1)} fusion(bf16[16,512,512]{2,1,0:T(8,128)(2,1)} %gather_fusion.4, pred[16]{0:T(512)(128)(4,1)S(1)} %get-tuple-element.61, bf16[16,512,128]{2,1,0:T(8,128)(2,1)S(1)} %gather_fusion.2), kind=kOutput, calls=%fused_computation.23 | convolution fusion | flops 1078984704 | bytes 12582928 | tf_op jit(solution)/shard_map/qxr,qxy->qry/dot_general | solution.py:66
  148.5 7.5 %fusion.27 = f32[16,128,128]{2,1,0:T(8,128)} fusion(bf16[1,16,512,512]{3,2,1,0:T(8,128)(2,1)} %param.19, bf16[16,512,128]{2,1,0:T(8,128)(2,1)} %gather_fusion.1, pred[16]{0:T(512)(128)(4,1)S(1)} %get-tuple-element.70, bf16[16,512,128]{2,1,0:T(8,128)(2,1)S(1)} %gather_fusion.2, pred[16]{0:T(512)(128)(4,1)S(1)} %get-tuple-element.61), kind=kOutput, calls=%fused_computation.39 | convolution fusion | flops 1345323008 | bytes 13631520 | tf_op jit(solution)/shard_map/qry,qys->qrs/dot_general | solution.py:75
  155.9 7.3 %fusion.44 = bf16[16,128,128]{2,1,0:T(8,128)(2,1)S(1)} fusion(f32[16,128,128]{2,1,0:T(8,128)} %fusion.27, bf16[16,128,512]{2,1,0:T(8,128)(2,1)} %fusion.16, bf16[16,512,512]{2,1,0:T(8,128)(2,1)} %gather_fusion.3, pred[16]{0:T(512)(128)(4,1)S(1)} %get-tuple-element.70, bf16[16,512,128]{2,1,0:T(8,128)(2,1)} %gather_fusion.1), kind=kOutput, calls=%fused_computation.46 | convolution fusion | flops 1348993024 | bytes 14155792 | tf_op jit(solution)/shard_map/qrk,qsk->qrs/dot_general | solution.py:76
  171.6 7.5 %gather_fusion.5 = bf16[64,512,128]{2,1,0:T(8,128)(2,1)} fusion(bf16[32,512,128]{2,1,0:T(8,128)(2,1)} %bitcast.80, s32[1024]{0:T(1024)S(1)} %pad_clamp_fusion.2), kind=kCustom, calls=%fused_computation.4.clone | custom fusion | bytes 16777472 | tf_op jit(solution)/shard_map/jit(_take)/gather | solution.py:113
  179.1 7.5 %gather_fusion = bf16[64,512,128]{2,1,0:T(8,128)(2,1)} fusion(bf16[32,512,128]{2,1,0:T(8,128)(2,1)} %bitcast.81, s32[1024]{0:T(1024)S(1)} %pad_clamp_fusion.5), kind=kCustom, calls=%fused_computation.clone | custom fusion | bytes 16777472 | tf_op jit(solution)/shard_map/jit(_take)/gather | solution.py:110
  186.6 7.5 %broadcast_select_fusion = bf16[64,512,128]{2,1,0:T(8,128)(2,1)} fusion(bf16[64,512,128]{2,1,0:T(8,128)(2,1)} %gather_fusion.5, pred[64]{0:T(512)(128)(4,1)S(1)} %get-tuple-element.74), kind=kLoop, calls=%fused_computation.27 | loop fusion | flops 4194304 | bytes 16777280 | tf_op jit(solution)/shard_map/jit(_take)/select_n | solution.py:113
  194.1 7.5 %broadcast_select_fusion.1 = bf16[64,512,128]{2,1,0:T(8,128)(2,1)} fusion(bf16[64,512,128]{2,1,0:T(8,128)(2,1)} %gather_fusion, pred[64]{0:T(512)(128)(4,1)S(1)} %get-tuple-element.75), kind=kLoop, calls=%fused_computation.30 | loop fusion | flops 4194304 | bytes 16777280 | tf_op jit(solution)/shard_map/jit(_take)/select_n | solution.py:110
  201.5 159.2 %while.10 = (s32[]{:T(128)}, f32[8,512,512]{2,1,0:T(8,128)}, s32[8,8]{1,0:T(8,128)S(1)}, bf16[8,8,512,128]{3,2,1,0:T(8,128)(2,1)}, bf16[8,8,128,128]{3,2,1,0:T(8...) while((s32[]{:T(128)}, f32[8,512,512]{2,1,0:T(8,128)}, s32[8,8]{1,0:T(8,128)S(1)}, ...), condition=%wide.region_9.13_spmd, body=%wide.region_7.12_spmd.sunk | while | flops 673710080 | bytes 35915440 | solution.py:128
  201.5 6.3 %fusion.88 = f32[8,512,512]{2,1,0:T(8,128)} fusion(bf16[8,8,512,128]{3,2,1,0:T(8,128)(2,1)} %get-tuple-element.136, s32[]{:T(128)} %get-tuple-element.124, bf16[8,8,512,128]{3,2,1,0:T(8,128)(2,1)} %get-tuple-element.134, bf16[8,8,128,128]{3,2,1,0:T(8,128)(2,1)S(1)} %get-tuple-element.135), kind=kOutput, calls=%fused_computation.11.clone.1 | convolution fusion | flops 671612928 | bytes 10749440 | tf_op jit(solution)/shard_map/while/body/eval_jaxpr/gxs,gys->gxy/dot_general | solution.py:123
  207.8 15.1 %scatter_fusion = f32[8,512,512]{2,1,0:T(8,128)} fusion(f32[8,512,512]{2,1,0:T(8,128)} %get-tuple-element.125, s32[8]{0:T(128)S(1)} %fusion.87, f32[8,512,512]{2,1,0:T(8,128)} %fusion.88), kind=kCustom, calls=%fused_computation.8.clone.1 | custom fusion | flops 2097152 | bytes 25165856 | tf_op jit(solution)/shard_map/while/body/eval_jaxpr/scatter-add | solution.py:126
  222.9 6.3 %fusion.88 = f32[8,512,512]{2,1,0:T(8,128)} fusion(bf16[8,8,512,128]{3,2,1,0:T(8,128)(2,1)} %get-tuple-element.136, s32[]{:T(128)} %get-tuple-element.124, bf16[8,8,512,128]{3,2,1,0:T(8,128)(2,1)} %get-tuple-element.134, bf16[8,8,128,128]{3,2,1,0:T(8,128)(2,1)S(1)} %get-tuple-element.135), kind=kOutput, calls=%fused_computation.11.clone.1 | convolution fusion | flops 671612928 | bytes 10749440 | tf_op jit(solution)/shard_map/while/body/eval_jaxpr/gxs,gys->gxy/dot_general | solution.py:123
  229.2 12.1 %scatter_fusion = f32[8,512,512]{2,1,0:T(8,128)} fusion(f32[8,512,512]{2,1,0:T(8,128)} %get-tuple-element.125, s32[8]{0:T(128)S(1)} %fusion.87, f32[8,512,512]{2,1,0:T(8,128)} %fusion.88), kind=kCustom, calls=%fused_computation.8.clone.1 | custom fusion | flops 2097152 | bytes 25165856 | tf_op jit(solution)/shard_map/while/body/eval_jaxpr/scatter-add | solution.py:126
  241.3 6.3 %fusion.88 = f32[8,512,512]{2,1,0:T(8,128)} fusion(bf16[8,8,512,128]{3,2,1,0:T(8,128)(2,1)} %get-tuple-element.136, s32[]{:T(128)} %get-tuple-element.124, bf16[8,8,512,128]{3,2,1,0:T(8,128)(2,1)} %get-tuple-element.134, bf16[8,8,128,128]{3,2,1,0:T(8,128)(2,1)S(1)} %get-tuple-element.135), kind=kOutput, calls=%fused_computation.11.clone.1 | convolution fusion | flops 671612928 | bytes 10749440 | tf_op jit(solution)/shard_map/while/body/eval_jaxpr/gxs,gys->gxy/dot_general | solution.py:123
  247.6 15.0 %scatter_fusion = f32[8,512,512]{2,1,0:T(8,128)} fusion(f32[8,512,512]{2,1,0:T(8,128)} %get-tuple-element.125, s32[8]{0:T(128)S(1)} %fusion.87, f32[8,512,512]{2,1,0:T(8,128)} %fusion.88), kind=kCustom, calls=%fused_computation.8.clone.1 | custom fusion | flops 2097152 | bytes 25165856 | tf_op jit(solution)/shard_map/while/body/eval_jaxpr/scatter-add | solution.py:126
  268.9 13.1 %scatter_fusion = f32[8,512,512]{2,1,0:T(8,128)} fusion(f32[8,512,512]{2,1,0:T(8,128)} %get-tuple-element.125, s32[8]{0:T(128)S(1)} %fusion.87, f32[8,512,512]{2,1,0:T(8,128)} %fusion.88), kind=kCustom, calls=%fused_computation.8.clone.1 | custom fusion | flops 2097152 | bytes 25165856 | tf_op jit(solution)/shard_map/while/body/eval_jaxpr/scatter-add | solution.py:126
  282.0 6.3 %fusion.88 = f32[8,512,512]{2,1,0:T(8,128)} fusion(bf16[8,8,512,128]{3,2,1,0:T(8,128)(2,1)} %get-tuple-element.136, s32[]{:T(128)} %get-tuple-element.124, bf16[8,8,512,128]{3,2,1,0:T(8,128)(2,1)} %get-tuple-element.134, bf16[8,8,128,128]{3,2,1,0:T(8,128)(2,1)S(1)} %get-tuple-element.135), kind=kOutput, calls=%fused_computation.11.clone.1 | convolution fusion | flops 671612928 | bytes 10749440 | tf_op jit(solution)/shard_map/while/body/eval_jaxpr/gxs,gys->gxy/dot_general | solution.py:123
  288.3 12.1 %scatter_fusion = f32[8,512,512]{2,1,0:T(8,128)} fusion(f32[8,512,512]{2,1,0:T(8,128)} %get-tuple-element.125, s32[8]{0:T(128)S(1)} %fusion.87, f32[8,512,512]{2,1,0:T(8,128)} %fusion.88), kind=kCustom, calls=%fused_computation.8.clone.1 | custom fusion | flops 2097152 | bytes 25165856 | tf_op jit(solution)/shard_map/while/body/eval_jaxpr/scatter-add | solution.py:126
  300.5 6.3 %fusion.88 = f32[8,512,512]{2,1,0:T(8,128)} fusion(bf16[8,8,512,128]{3,2,1,0:T(8,128)(2,1)} %get-tuple-element.136, s32[]{:T(128)} %get-tuple-element.124, bf16[8,8,512,128]{3,2,1,0:T(8,128)(2,1)} %get-tuple-element.134, bf16[8,8,128,128]{3,2,1,0:T(8,128)(2,1)S(1)} %get-tuple-element.135), kind=kOutput, calls=%fused_computation.11.clone.1 | convolution fusion | flops 671612928 | bytes 10749440 | tf_op jit(solution)/shard_map/while/body/eval_jaxpr/gxs,gys->gxy/dot_general | solution.py:123
  306.8 13.2 %scatter_fusion = f32[8,512,512]{2,1,0:T(8,128)} fusion(f32[8,512,512]{2,1,0:T(8,128)} %get-tuple-element.125, s32[8]{0:T(128)S(1)} %fusion.87, f32[8,512,512]{2,1,0:T(8,128)} %fusion.88), kind=kCustom, calls=%fused_computation.8.clone.1 | custom fusion | flops 2097152 | bytes 25165856 | tf_op jit(solution)/shard_map/while/body/eval_jaxpr/scatter-add | solution.py:126
  320.0 6.3 %fusion.88 = f32[8,512,512]{2,1,0:T(8,128)} fusion(bf16[8,8,512,128]{3,2,1,0:T(8,128)(2,1)} %get-tuple-element.136, s32[]{:T(128)} %get-tuple-element.124, bf16[8,8,512,128]{3,2,1,0:T(8,128)(2,1)} %get-tuple-element.134, bf16[8,8,128,128]{3,2,1,0:T(8,128)(2,1)S(1)} %get-tuple-element.135), kind=kOutput, calls=%fused_computation.11.clone.1 | convolution fusion | flops 671612928 | bytes 10749440 | tf_op jit(solution)/shard_map/while/body/eval_jaxpr/gxs,gys->gxy/dot_general | solution.py:123
  326.2 15.1 %scatter_fusion = f32[8,512,512]{2,1,0:T(8,128)} fusion(f32[8,512,512]{2,1,0:T(8,128)} %get-tuple-element.125, s32[8]{0:T(128)S(1)} %fusion.87, f32[8,512,512]{2,1,0:T(8,128)} %fusion.88), kind=kCustom, calls=%fused_computation.8.clone.1 | custom fusion | flops 2097152 | bytes 25165856 | tf_op jit(solution)/shard_map/while/body/eval_jaxpr/scatter-add | solution.py:126
  341.3 6.3 %fusion.88 = f32[8,512,512]{2,1,0:T(8,128)} fusion(bf16[8,8,512,128]{3,2,1,0:T(8,128)(2,1)} %get-tuple-element.136, s32[]{:T(128)} %get-tuple-element.124, bf16[8,8,512,128]{3,2,1,0:T(8,128)(2,1)} %get-tuple-element.134, bf16[8,8,128,128]{3,2,1,0:T(8,128)(2,1)S(1)} %get-tuple-element.135), kind=kOutput, calls=%fused_computation.11.clone.1 | convolution fusion | flops 671612928 | bytes 10749440 | tf_op jit(solution)/shard_map/while/body/eval_jaxpr/gxs,gys->gxy/dot_general | solution.py:123
  347.6 13.1 %scatter_fusion = f32[8,512,512]{2,1,0:T(8,128)} fusion(f32[8,512,512]{2,1,0:T(8,128)} %get-tuple-element.125, s32[8]{0:T(128)S(1)} %fusion.87, f32[8,512,512]{2,1,0:T(8,128)} %fusion.88), kind=kCustom, calls=%fused_computation.8.clone.1 | custom fusion | flops 2097152 | bytes 25165856 | tf_op jit(solution)/shard_map/while/body/eval_jaxpr/scatter-add | solution.py:126
  375.0 9.6 %scatter_fusion.1 = f32[32,512,128]{2,1,0:T(8,128)} fusion(f32[32,512,128]{2,1,0:T(8,128)} %broadcast.101, s32[16]{0:T(128)S(1)} %add_bitcast_fusion, f32[16,512,128]{2,1,0:T(8,128)} %pad_maximum_fusion), kind=kCustom, calls=%fused_computation.9 | custom fusion | flops 1048576 | bytes 12582976 | tf_op jit(solution)/shard_map/add | solution.py:151
  388.6 53.8 %all_to_all.15 = bf16[4,4096,128]{2,1,0:T(8,128)(2,1)} all-to-all(bf16[4,4096,128]{2,1,0:T(8,128)(2,1)S(1)} %bitcast.86), channel_id=1, replica_groups=mesh['child'=4,'tile'=32] {'child'}, dimensions={0} | all-to-all | bytes 8388608 | tf_op jit(solution)/shard_map/all_to_all | solution.py:28
  446.5 13.5 %all-to-all-start.2 = ((bf16[32,128,128]{2,1,0:T(8,128)(2,1)}), bf16[32,128,128]{2,1,0:T(8,128)(2,1)S(1)}, u32[]{:S(2)}, u32[]{:S(2)}) async-start(bf16[32,128,128]{2,1,0:T(8,128)(2,1)} %bitcast.29), calls=%async_computation.2 | async-start | bytes 2097152 | tf_op jit(solution)/shard_map/all_to_all | solution.py:28
  466.0 10.9 %all-to-all-done.2 = bf16[32,128,128]{2,1,0:T(8,128)(2,1)S(1)} async-done(((bf16[32,128,128]{2,1,0:T(8,128)(2,1)}), bf16[32,128,128]{2,1,0:T(8,128)(2,1)S(1)}, u32[]{:S(2)}, u32[]{:S(2)}) %all-to-all-start.2) | async-done | bytes 1048608 | tf_op jit(solution)/shard_map/all_to_all | solution.py:28
  (74 shorter events, 71.2 us)
Async XLA Ops:
  7.2 15.2 %copy-start.1 = (s32[1,8,2]{1,2,0:T(2,128)S(1)}, s32[1,8,2]{1,2,0:T(2,128)}, u32[]{:S(2)}) copy-start(s32[1,8,2]{1,2,0:T(2,128)} %param.26) | copy-start | bytes 196
  7.2 88.6 %all-gather.2.cloned.1.call-start = ((), (), s32[]{:S(2)}) async-start(), calls=%async_computation.3 | async-start | bytes 21626880 | tf_op jit(solution)/shard_map/all_gather | solution.py:13
  166.2 35.3 %all-to-all-start = ((bf16[32,2,128,128]{3,2,1,0:T(8,128)(2,1)}), bf16[32,2,128,128]{3,2,1,0:T(8,128)(2,1)S(1)}, u32[]{:S(2)}, u32[]{:S(2)}) async-start(bf16[32,2,128,128]{3,2,1,0:T(8,128)(2,1)} %copy.34), calls=%async_computation | async-start | bytes 4194304 | tf_op jit(solution)/shard_map/all_to_all | solution.py:92
  360.7 6.1 %copy-start = (f32[8,512,512]{2,1,0:T(8,128)S(1)}, f32[8,512,512]{2,1,0:T(8,128)}, u32[]{:S(2)}) copy-start(f32[8,512,512]{2,1,0:T(8,128)} %get-tuple-element.38) | copy-start | bytes 25165828
  446.5 30.3 %all-to-all-start.2 = ((bf16[32,128,128]{2,1,0:T(8,128)(2,1)}), bf16[32,128,128]{2,1,0:T(8,128)(2,1)S(1)}, u32[]{:S(2)}, u32[]{:S(2)}) async-start(bf16[32,128,128]{2,1,0:T(8,128)(2,1)} %bitcast.29), calls=%async_computation.2 | async-start | bytes 2097152 | tf_op jit(solution)/shard_map/all_to_all | solution.py:28
Sparse Core Ops, SparseCore 0:
  10.8 84.9 all-gather.1
where the time goes:
time: 487 us; the launch traced here: 484 us
  other arithmetic  164 us (34%)
  matrix products  79.1 us (16%)
  local copies, waits for them, and re-layouts  78.5 us (16%)
  waiting for transfers between devices  76.3 us (16%)
  blocking collectives  53.8 us (11%)
  starting transfers between devices  18.9 us (4%)
  between operations  14.2 us (3%)
    scatter-add x8, other arithmetic, decode(): jax.ops.segment_sum(decoded, slot_group, num_segments=parent_count)  109 us
    all_gather x1, waiting for transfers between devices, in_one_piece(): lax.all_gather(both, axis, axis=dim, tiled=True)  65.4 us
    all_to_all x1, blocking collectives, sum_at_owner(): parts = lax.all_to_all(cut_along(shard, dim, size), axis, 0, 0, tiled=True)  53.8 us
    dot_general x8, matrix products, decode(): jnp.einsum('gxs,gys->gxy', left_part, right_group, preferred_element_type...  50.2 us
    slice x2, local copies, waits for them, and re-layouts, in_one_piece(): finished.append(lax.slice_in_dim(out, at, at + a.shape[along], axis=along))  17.6 us
    all_to_all x1, starting transfers between devices, sum_at_owner(): parts = lax.all_to_all(cut_along(shard, dim, size), axis, 0, 0, tiled=True)  13.5 us
    all_to_all x1, waiting for transfers between devices, sum_at_owner(): parts = lax.all_to_all(cut_along(shard, dim, size), axis, 0, 0, tiled=True)  10.9 us
    gather x1, local copies, waits for them, and re-layouts, shards(): jnp.take(panel_blocks, row_ids, axis=0)  10.5 us
  transfers between devices with their start and end apart: 3, of which 2 were waited for; matrix products, arithmetic and copies ran while one was open for 12% of the time, Pallas kernels for 0%

commit v1 on v0

v1 whole, which is shorter than its diff:
```python
import functools

import jax
import jax.numpy as jnp
from jax import lax
from jax.experimental import pallas as pl
from jax.experimental.pallas import tpu as pltpu
from jax.sharding import PartitionSpec as P

CAP = 2
SIDE = 4
F32 = jnp.float32
BF16 = jnp.bfloat16
SPLIT = ((0, 48), (48, 48), (96, 32))
ORDERS = ((0, 1, 2), (1, 2, 0), (2, 0, 1))


def dot(a, b, ca, cb):
    return lax.dot_general(a, b, (((ca,), (cb,)), ((), ())), preferred_element_type=F32)


def shift(p, by):
    return lax.rem(p + by + SIDE, SIDE)


def greet(devices):
    barrier = pltpu.get_barrier_semaphore()
    for device in devices:
        pl.semaphore_signal(barrier, inc=1, device_id=device)


def await_greetings(count):
    pl.semaphore_wait(pltpu.get_barrier_semaphore(), count)


def route_kernel(
    owners,
    idx_ref,
    panel_hbm,
    bases_hbm,
    tiles_hbm,
    bases_out,
    cores_out,
    table_ref,
    tiles,
    panel,
    bases,
    proj,
    cores,
    outgoing,
    load_sem,
    own_sem,
    send_sem,
    recv_sem,
    a2a_send,
    a2a_recv,
):
    t = lax.axis_index("tile")
    x, z, c = t // 8, lax.rem(t // 2, SIDE), lax.rem(t, 2)
    count = tiles.shape[0]

    load_panel = pltpu.make_async_copy(panel_hbm, panel, load_sem.at[0])
    load_bases = pltpu.make_async_copy(bases_hbm, bases.at[t], load_sem.at[1])
    load_tiles = pltpu.make_async_copy(tiles_hbm, tiles, load_sem.at[2])
    load_panel.start()
    load_bases.start()
    load_tiles.start()

    @pl.loop(1, owners)
    def _(step):
        pl.semaphore_signal(
            pltpu.get_barrier_semaphore(),
            inc=1,
            device_id={"tile": lax.rem(t + step, owners)},
        )

    load_panel.wait()
    load_bases.wait()
    proj[t] = dot(bases[t], panel[...], 0, 0).astype(BF16)
    await_greetings(owners - 1)

    def along_x(first, second):
        return first * 8 + second * 2 + c

    def along_z(first, second):
        return second * 8 + first * 2 + c

    sibling = t + 1 - 2 * c
    pending = []

    class Gather:
        def __init__(self, buf, number, first, second, device):
            self.buf, self.n, self.f, self.s, self.dev = buf, number, first, second, device
            self.half = buf.shape[1] // 2

        def copy(self, block, half, peer, k):
            ref = self.buf.at[block]
            if half is not None:
                ref = ref.at[pl.ds(half * self.half, self.half)]
            return pltpu.make_async_remote_copy(
                src_ref=ref,
                dst_ref=ref,
                send_sem=send_sem.at[self.n, k],
                recv_sem=recv_sem.at[self.n, k],
                device_id={"tile": peer},
            )

        def send(self, block, half, peer, k):
            copy = self.copy(block, half, peer, k)
            copy.start()
            pending.append(copy)

        def to_sibling(self, block, k):
            self.send(block, None, sibling, 20 + k)

        def open_ring(self, ring, place):
            block, up, down = place(0), place(1, True), place(-1, True)
            self.send(block, None, up, 4 * ring)
            self.send(block, None, down, 4 * ring + 1)

        def relay_up(self, ring, place):
            block = place(-1)
            self.copy(block, None, place(-1, True), 4 * ring).wait_recv()
            self.send(block, 0, place(1, True), 4 * ring + 2)
            return block

        def relay_down(self, ring, place):
            block = place(1)
            self.copy(block, None, place(1, True), 4 * ring + 1).wait_recv()
            self.send(block, 1, place(-1, True), 4 * ring + 3)
            return block

        def close_ring(self, ring, place):
            block = place(2)
            self.copy(block, 0, place(-1, True), 4 * ring + 2).wait_recv()
            self.copy(block, 1, place(1, True), 4 * ring + 3).wait_recv()
            return block

        def first_ring(self):
            def place(by, device=False):
                return self.dev(shift(self.f, by), self.s)

            return place

        def second_ring(self, offset):
            def place(by, device=False):
                first = self.f if device else shift(self.f, offset)
                return self.dev(first, shift(self.s, by))

            return place

    both = (Gather(bases, 0, x, z, along_x), Gather(proj, 1, z, x, along_z))
    offsets = (None, 0, -1, 1, 2)
    seconds = [[g.second_ring(o) if o is not None else None for o in offsets] for g in both]
    for g, s in zip(both, seconds):
        g.open_ring(0, g.first_ring())
        g.open_ring(1, s[1])
        g.to_sibling(t, 0)
    for g, s in zip(both, seconds):
        g.to_sibling(g.relay_up(0, g.first_ring()), 1)
        g.open_ring(2, s[2])
        g.to_sibling(g.relay_down(0, g.first_ring()), 2)
        g.open_ring(3, s[3])
    for g, s in zip(both, seconds):
        g.to_sibling(g.relay_up(1, s[1]), 3)
        g.to_sibling(g.relay_down(1, s[1]), 4)
    for g, s in zip(both, seconds):
        g.to_sibling(g.close_ring(0, g.first_ring()), 5)
        g.open_ring(4, s[4])
    for ring in (2, 3):
        for g, s in zip(both, seconds):
            g.to_sibling(g.relay_up(ring, s[ring]), 2 * ring + 2)
            g.to_sibling(g.relay_down(ring, s[ring]), 2 * ring + 3)
    for g, s in zip(both, seconds):
        g.to_sibling(g.close_ring(1, s[1]), 10)
    for g, s in zip(both, seconds):
        g.to_sibling(g.relay_up(4, s[4]), 11)
        g.to_sibling(g.relay_down(4, s[4]), 12)
    for ring in (2, 3, 4):
        for g, s in zip(both, seconds):
            g.to_sibling(g.close_ring(ring, s[ring]), 11 + ring)
    for g, s in zip(both, seconds):
        first = g.first_ring()
        order = [
            first(0), first(-1), first(1), s[1](-1), s[1](1), first(2),
            s[2](-1), s[2](1), s[3](-1), s[3](1), s[1](2), s[4](-1), s[4](1),
            s[2](2), s[3](2), s[4](2),
        ]
        for k, block in enumerate(order):
            g.copy(block + 1 - 2 * c, None, sibling, 20 + k).wait_recv()
    for copy in pending:
        copy.wait_send()

    keep_bases = pltpu.make_async_copy(bases, bases_out, own_sem.at[0])
    keep_bases.start()
    load_tiles.wait()

    @pl.loop(0, count)
    def _(q):
        entry = idx_ref[t * count + q]
        i, j = entry & 255, (entry >> 8) & 255
        half = dot(bases[i], tiles[q], 0, 0).astype(BF16)
        core = dot(half, bases[j], 1, 0) - dot(proj[i], proj[j], 1, 1)
        cores[q] = core.astype(BF16)

    dests = [idx_ref[t * count + q] >> 24 for q in range(count)]

    def outbound(step, target):
        return pltpu.make_async_remote_copy(
            src_ref=outgoing.at[step],
            dst_ref=cores_out.at[t],
            send_sem=a2a_send.at[step],
            recv_sem=a2a_recv.at[step],
            device_id={"tile": target},
        )

    def pack(step, target):
        first, last = jnp.int32(0), jnp.int32(0)
        for q in range(count):
            last = jnp.where(dests[q] == target, q, last)
            back = count - 1 - q
            first = jnp.where(dests[back] == target, back, first)
        outgoing[step, 0] = cores[first]
        outgoing[step, 1] = cores[last]

    @pl.loop(1, owners)
    def _(step):
        target = lax.rem(t + step, owners)
        pack(step, target)
        outbound(step, target).start()

    pack(0, t)
    keep_own = pltpu.make_async_copy(outgoing.at[0], cores_out.at[t], own_sem.at[1])
    keep_own.start()

    @pl.loop(0, owners)
    def _(source):
        first, last, found = jnp.int32(0), jnp.int32(0), jnp.int32(0)
        for q in range(count):
            entry = idx_ref[source * count + q]
            hit = (entry >> 24) == t
            last = jnp.where(hit, entry, last)
            first = jnp.where(hit & (found == 0), entry, first)
            found = found + hit.astype(jnp.int32)
        table_ref[source * CAP] = jnp.where(found > 0, first, -1)
        table_ref[source * CAP + 1] = jnp.where(found > 1, last, -1)

    @pl.loop(1, owners)
    def _(step):
        source = lax.rem(t - step + owners, owners)
        pltpu.make_async_remote_copy(
            src_ref=outgoing.at[step],
            dst_ref=cores_out.at[source],
            send_sem=a2a_send.at[step],
            recv_sem=a2a_recv.at[step],
            device_id={"tile": source},
        ).wait()

    keep_own.wait()
    keep_bases.wait()


def decode_kernel(
    table_ref,
    pblocks_ref,
    bases_hbm,
    cores_hbm,
    parents_hbm,
    test_hbm,
    updated_hbm,
    sketch_hbm,
    bases,
    cores,
    parents,
    test,
    total,
    part,
    rounded,
    load_sem,
    tile_sem,
    store_sem,
):
    held = parents.shape[0]
    blocks = part.shape[0]
    loads = [
        pltpu.make_async_copy(bases_hbm, bases, load_sem.at[0]),
        pltpu.make_async_copy(cores_hbm, cores, load_sem.at[1]),
    ]
    tiles = [
        pltpu.make_async_copy(parents_hbm.at[p], parents.at[p], tile_sem.at[p])
        for p in range(held)
    ]
    load_test = pltpu.make_async_copy(test_hbm, test, load_sem.at[2])
    for copy in tiles + loads + [load_test]:
        copy.start()

    @pl.loop(0, blocks)
    def _(b):
        part[b] = jnp.zeros_like(part[b])

    for p in range(held):
        tiles[p].wait()
        total[p] = parents[p].astype(F32)
    for copy in loads:
        copy.wait()

    @pl.loop(0, cores.shape[0])
    def _(k):
        entry = table_ref[k]

        @pl.when(entry >= 0)
        def _():
            i, j, slot = entry & 255, (entry >> 8) & 255, (entry >> 16) & 255
            left = dot(bases[i], cores[k], 1, 0).astype(BF16)
            total[slot] += dot(left, bases[j], 1, 1)

    load_test.wait()
    stores = []
    for p in range(held):
        a, b = pblocks_ref[2 * p], pblocks_ref[2 * p + 1]
        new = total[p].astype(BF16)
        parents[p] = new
        store = pltpu.make_async_copy(parents.at[p], updated_hbm.at[p], tile_sem.at[p])
        store.start()
        stores.append(store)
        part[a] += dot(new, test[b], 1, 0)

        @pl.when(a != b)
        def _():
            part[b] += dot(new, test[a], 0, 0)

    groups = 4
    size = blocks // groups
    for g in range(groups):
        span = pl.ds(g * size, size)
        rounded[span] = part[span].astype(BF16)
        store = pltpu.make_async_copy(rounded.at[span], sketch_hbm.at[span], store_sem.at[g])
        store.start()
        stores.append(store)
    for store in stores:
        store.wait()


def reduce_kernel(part_hbm, out_ref, *scratch):
    n = len(SPLIT)
    mine, heard, held = scratch[:n], scratch[n : 2 * n], scratch[2 * n : 3 * n]
    got1, held2, got2, held3, got3 = (scratch[(3 + i) * n : (4 + i) * n] for i in range(5))
    own_sem, send_sem, recv_sem = scratch[8 * n :]
    y, t = lax.axis_index("child"), lax.axis_index("tile")
    x, z, c = t // 8, lax.rem(t // 2, SIDE), lax.rem(t, 2)
    here = (y, x, z)

    def device(coords, core):
        return {"child": coords[0], "tile": coords[1] * 8 + coords[2] * 2 + core}

    def moved(axis, by):
        return tuple(shift(p, by) if a == axis else p for a, p in enumerate(here))

    sibling = device(here, 1 - c)
    greet([sibling] + [device(moved(a, by), c) for a in range(3) for by in (1, 2, 3)])

    own = []
    for k, (at, rows) in enumerate(SPLIT):
        copy = pltpu.make_async_copy(
            part_hbm.at[:, :, :, c, pl.ds(at, rows)], mine[k], own_sem.at[k]
        )
        copy.start()
        own.append(copy)
    await_greetings(10)

    pending = []

    def remote(src, dst, number, peer):
        copy = pltpu.make_async_remote_copy(
            src_ref=src,
            dst_ref=dst,
            send_sem=send_sem.at[number],
            recv_sem=recv_sem.at[number],
            device_id=peer,
        )
        pending.append(copy)
        copy.start()
        return copy

    swaps = [
        remote(part_hbm.at[:, :, :, 1 - c, pl.ds(at, rows)], heard[k], 30 + k, sibling)
        for k, (at, rows) in enumerate(SPLIT)
    ]

    def pick(ref, axis, which):
        return ref.at[(slice(None),) * axis + (which,)]

    def left_axes(k, stage):
        axes = [a for a in range(3) if a not in ORDERS[k][:stage]]
        return axes.index(ORDERS[k][stage])

    def scatter(k, stage, buf, got):
        axis, copies = ORDERS[k][stage], []
        at = left_axes(k, stage)
        for by in (1, 3, 2):
            copies.append(
                remote(
                    pick(buf, at, shift(here[axis], by)),
                    got.at[by - 1],
                    9 * k + 3 * stage + by - 1,
                    device(moved(axis, by), c),
                )
            )
        return copies

    def gather_up(k, stage, buf, got, copies, dst):
        axis = ORDERS[k][stage]
        for copy in copies:
            copy.wait_recv()
        kept = pick(buf, left_axes(k, stage), here[axis])[...].astype(F32)
        value = kept + got[0].astype(F32) + got[1].astype(F32) + got[2].astype(F32)
        dst[...] = value.astype(dst.dtype)

    flying = []
    for k in range(n):
        own[k].wait()
        swaps[k].wait_recv()

        @pl.loop(0, SIDE)
        def _(a):
            held[k][a] = (mine[k][a].astype(F32) + heard[k][a].astype(F32)).astype(BF16)

        flying.append(scatter(k, 0, held[k], got1[k]))
    for k in range(n):
        gather_up(k, 0, held[k], got1[k], flying[k], held2[k])
        flying[k] = scatter(k, 1, held2[k], got2[k])
    for k in range(n):
        gather_up(k, 1, held2[k], got2[k], flying[k], held3[k])
        flying[k] = scatter(k, 2, held3[k], got3[k])
    for k, (at, rows) in enumerate(SPLIT):
        gather_up(k, 2, held3[k], got3[k], flying[k], out_ref.at[pl.ds(at, rows)])
    for copy in pending:
        copy.wait_send()


def shards(
    child_tiles,
    panel,
    bases,
    tile_blocks,
    tile_dest,
    tile_slot,
    parent_tiles,
    parent_blocks,
    sketch_test,
):
    owners = lax.axis_size("tile")
    _, count, order, _ = child_tiles.shape
    rank = bases.shape[2]
    width = sketch_test.shape[1]
    held = parent_tiles.shape[1]
    blocks = sketch_test.shape[0] // order
    chunk = sketch_test.shape[0] // (SIDE**3 * 2)
    any_space = pl.BlockSpec(memory_space=pl.ANY)
    smem = pl.BlockSpec(memory_space=pltpu.SMEM)
    vmem = pl.BlockSpec(memory_space=pltpu.VMEM)
    dma = pltpu.SemaphoreType.DMA

    packed = (
        tile_blocks[0, :, 0]
        + tile_blocks[0, :, 1] * 256
        + tile_slot[0] * 65536
        + tile_dest[0, :, 0] * 16777216
    )
    whole_bases, cores, table = pl.pallas_call(
        functools.partial(route_kernel, owners),
        out_shape=(
            jax.ShapeDtypeStruct((owners, order, rank), BF16),
            jax.ShapeDtypeStruct((owners, CAP, rank, rank), BF16),
            jax.ShapeDtypeStruct((owners * CAP,), jnp.int32),
        ),
        in_specs=[smem, any_space, any_space, any_space],
        out_specs=(any_space, any_space, smem),
        scratch_shapes=[
            pltpu.VMEM((count, order, order), BF16),
            pltpu.VMEM((order, order), BF16),
            pltpu.VMEM((owners, order, rank), BF16),
            pltpu.VMEM((owners, rank, order), BF16),
            pltpu.VMEM((count, rank, rank), BF16),
            pltpu.VMEM((owners, CAP, rank, rank), BF16),
            dma((3,)),
            dma((2,)),
            dma((2, 36)),
            dma((2, 36)),
            dma((owners,)),
            dma((owners,)),
        ],
        compiler_params=pltpu.CompilerParams(
            collective_id=0, has_side_effects=True, vmem_limit_bytes=40 << 20
        ),
        name="encode_and_route",
    )(packed, panel[0], bases[0], child_tiles[0])

    updated, part = pl.pallas_call(
        decode_kernel,
        out_shape=(
            jax.ShapeDtypeStruct((held, order, order), BF16),
            jax.ShapeDtypeStruct((blocks, order, width), BF16),
        ),
        in_specs=[smem, smem, any_space, any_space, any_space, any_space],
        out_specs=(any_space, any_space),
        scratch_shapes=[
            pltpu.VMEM((owners, order, rank), BF16),
            pltpu.VMEM((owners * CAP, rank, rank), BF16),
            pltpu.VMEM((held, order, order), BF16),
            pltpu.VMEM((blocks, order, width), BF16),
            pltpu.VMEM((held, order, order), F32),
            pltpu.VMEM((blocks, order, width), F32),
            pltpu.VMEM((blocks, order, width), BF16),
            dma((3,)),
            dma((held,)),
            dma((4,)),
        ],
        compiler_params=pltpu.CompilerParams(vmem_limit_bytes=52 << 20),
        name="decode_and_sketch",
    )(
        table,
        parent_blocks.reshape(-1),
        whole_bases,
        cores.reshape(owners * CAP, rank, rank),
        parent_tiles[0],
        sketch_test.reshape(blocks, order, width),
    )

    def bufs(*lead):
        return [pltpu.VMEM((*lead, rows, width), BF16) for _, rows in SPLIT]

    row_sketch = pl.pallas_call(
        reduce_kernel,
        out_shape=jax.ShapeDtypeStruct((chunk, width), F32),
        in_specs=[any_space],
        out_specs=vmem,
        scratch_shapes=[
            *bufs(4, 4, 4),
            *bufs(4, 4, 4),
            *bufs(4, 4, 4),
            *bufs(3, 4, 4),
            *bufs(4, 4),
            *bufs(3, 4),
            *bufs(4),
            *bufs(3),
            dma((3,)),
            dma((33,)),
            dma((33,)),
        ],
        compiler_params=pltpu.CompilerParams(
            collective_id=1, has_side_effects=True, vmem_limit_bytes=32 << 20
        ),
        name="reduce_sketch",
    )(part.reshape(SIDE, SIDE, SIDE, 2, chunk, width))
    return (updated[None], row_sketch)


def solution(mesh):
    return jax.shard_map(
        shards,
        mesh=mesh,
        in_specs=(
            P("child", "tile", None, None),
            P("child", "tile", None),
            P("child", "tile", None),
            P("child", None, None),
            P("child", None, None),
            P("child", None),
            P("child", "tile", None, None),
            P("child", "tile", None),
            P(),
        ),
        out_specs=(P("child", "tile", None, None), P(("child", "tile"), None)),
        check_vma=False,
    )
```

time: 487 us -> 154 us (0.32)
  other arithmetic: 164 us -> 2.14 us
  Pallas kernels: 0 us -> 142 us
  matrix products: 79.1 us -> 0 us
  waiting for transfers between devices: 76.3 us -> 0 us
  local copies, waits for them, and re-layouts: 78.5 us -> 8.89 us
  blocking collectives: 53.8 us -> 0 us
  starting transfers between devices: 18.9 us -> 0 us
  between operations: 14.2 us -> 0.68 us
    pallas_call x0 -> x3, Pallas kernels: none -> 142 us  [the longest x1 73.3 us: shards(): pl.pallas_call(functools.partial(route_kernel, owners), out_shape=(jax.Sh...]
    scatter-add x8 -> x0, other arithmetic: 109 us -> none  [decode(): jax.ops.segment_sum(decoded, slot_group, num_segments=parent_count)]
    dot_general x14 -> x0, matrix products: 79.1 us -> none  [the longest x8 50.2 us: decode(): jnp.einsum('gxs,gys->gxy', left_part, right_group, preferred_element_type...]
    all_gather x1 -> x0, waiting for transfers between devices: 65.4 us -> none  [in_one_piece(): lax.all_gather(both, axis, axis=dim, tiled=True)]
    all_to_all x1 -> x0, blocking collectives: 53.8 us -> none  [sum_at_owner(): parts = lax.all_to_all(cut_along(shard, dim, size), axis, 0, 0, tiled=True)]
    gather x8 -> x0, local copies, waits for them, and re-layouts: 50.2 us -> none  [the longest x1 10.5 us: shards(): jnp.take(panel_blocks, row_ids, axis=0)]
    all_to_all x2 -> x0, starting transfers between devices: 18.9 us -> none  [the longest x1 13.5 us: sum_at_owner(): parts = lax.all_to_all(cut_along(shard, dim, size), axis, 0, 0, tiled=True)]
    slice x3 -> x0, local copies, waits for them, and re-layouts: 18.3 us -> none  [the longest x2 17.6 us: in_one_piece(): finished.append(lax.slice_in_dim(out, at, at + a.shape[along], axis=along))]
  transfers between devices with their start and end apart: 3 -> 0, of which waited for: 2 -> 0; matrix products, arithmetic and copies ran while one was open for 12% -> 0% of each run, Pallas kernels for 0% -> 0%
where the time goes in v1:
time: 154 us; the launch traced here: 153 us
  Pallas kernels  142 us (92%)
  local copies, waits for them, and re-layouts  8.89 us (6%)
  other arithmetic  2.14 us (1%)
    pallas_call x1, Pallas kernels, shards(): pl.pallas_call(functools.partial(route_kernel, owners), out_shape=(jax.Sh...  73.3 us
    pallas_call x1, Pallas kernels, shards(): pl.pallas_call(reduce_kernel, out_shape=jax.ShapeDtypeStruct((chunk, widt...  51 us
    pallas_call x1, Pallas kernels, shards(): pl.pallas_call(decode_kernel, out_shape=(jax.ShapeDtypeStruct((held, orde...  17.2 us
    unnamed x12, local copies, waits for them, and re-layouts  8.81 us

profile of v1, /device:TPU:0, one launch (start us, length us, event | category | flops | bytes accessed | tf_op | source)
XLA Modules:
  0.0 153.2 jit_solution(17338211317479789240)
XLA Ops:
  0.6 0.8 multiply_add_fusion
  1.4 0.7 broadcast_multiply_fusion
  2.1 0.7 broadcast_multiply_fusion.1
  2.8 0.8 copy.12
  3.5 0.1 reshape.23.pblocks_ref
  3.6 0.0 copy-start.3
  3.6 1.0 copy-done.3
  4.7 0.0 copy-start.4
  4.7 0.9 copy-done.4
  5.6 73.3 %encode_and_route.1 = (bf16[32,512,128]{2,1,0:T(8,128)(2,1)S(1)}, bf16[32,2,128,128]{3,2,1,0:T(8,128)(2,1)S(1)}, s32[64]{0:T(128)S(1)}) custom-call(s32[512]{0:T(512)S(1)} %add_add_fusion.idx_ref, bf16[512,512]{1,0:T(8,128)(2,1)S(1)} %bitcast.13, bf16[512,128]{1,0:T(8,128)(2,1)S(1)} %bitcast.14, bf16[16,512,512]{2,1,0:T(8,128)(2,1)} %bitcast.15), custom_call_target="tpu_custom_call" | custom-call | tf_op jit(solution)/shard_map/encode_and_route/pallas_call | solution.py:470
  78.9 0.0 copy-start.1
  78.9 1.9 %copy-done.1 = bf16[32,512,128]{2,1,0:T(8,128)(2,1)} copy-done((bf16[32,512,128]{2,1,0:T(8,128)(2,1)}, bf16[32,512,128]{2,1,0:T(8,128)(2,1)S(1)}, u32[]{:S(2)}) %copy-start.1) | copy-done | bytes 4194328
  80.8 0.0 copy-start.2
  80.8 1.4 copy-done.2
  82.2 17.2 %decode_and_sketch.1 = (bf16[8,512,512]{2,1,0:T(8,128)(2,1)}, bf16[32,512,128]{2,1,0:T(8,128)(2,1)}) custom-call(s32[64]{0:T(128)S(1)} %get-tuple-element.7.table_ref, s32[16]{0:T(128)S(1)} %reshape.23.pblocks_ref, bf16[32,512,128]{2,1,0:T(8,128)(2,1)} %copy-done.1, bf16[64,128,128]{2,1,0:T(8,128)(2,1)} %bitcast.12, bf16[8,512,512]{2,1,0:T(8,128)(2,1)} %bitcast.16, ...), custom_call_target="tpu_custom_call" | custom-call | tf_op jit(solution)/shard_map/decode_and_sketch/pallas_call | solution.py:499
  99.4 0.0 copy-start
  99.4 2.2 %copy-done = bf16[32,512,128]{2,1,0:T(8,128)(2,1)S(1)} copy-done((bf16[32,512,128]{2,1,0:T(8,128)(2,1)S(1)}, bf16[32,512,128]{2,1,0:T(8,128)(2,1)}, u32[]{:S(2)}) %copy-start) | copy-done | bytes 4194328
  101.6 51.0 %reduce_sketch.1 = f32[128,128]{1,0:T(8,128)S(1)} custom-call(bf16[4,4,4,2,128,128]{5,4,3,2,1,0:T(8,128)(2,1)S(1)} %bitcast.11), custom_call_target="tpu_custom_call" | custom-call | tf_op jit(solution)/shard_map/reduce_sketch/pallas_call | solution.py:533
  152.6 0.6 copy.14
  (1 shorter events, 0.0 us)
Async XLA Ops:
  3.6 1.0 copy-start.3
  4.7 0.9 copy-start.4
  78.9 1.9 %copy-start.1 = (bf16[32,512,128]{2,1,0:T(8,128)(2,1)}, bf16[32,512,128]{2,1,0:T(8,128)(2,1)S(1)}, u32[]{:S(2)}) copy-start(bf16[32,512,128]{2,1,0:T(8,128)(2,1)S(1)} %get-tuple-element.8.bases_hbm) | copy-start | bytes 12582916
  80.8 1.4 copy-start.2
  99.4 2.2 %copy-start = (bf16[32,512,128]{2,1,0:T(8,128)(2,1)S(1)}, bf16[32,512,128]{2,1,0:T(8,128)(2,1)}, u32[]{:S(2)}) copy-start(bf16[32,512,128]{2,1,0:T(8,128)(2,1)} %get-tuple-element.11) | copy-start | bytes 12582916

commit v2 on v1

v2 whole, which is shorter than its diff:
```python
import functools

import jax
import jax.numpy as jnp
from jax import lax
from jax.experimental import pallas as pl
from jax.experimental.pallas import tpu as pltpu
from jax.sharding import PartitionSpec as P

CAP = 2
SIDE = 4
F32 = jnp.float32
BF16 = jnp.bfloat16
SPLIT = ((0, 48), (48, 48), (96, 32))
ORDERS = ((0, 1, 2), (1, 2, 0), (2, 0, 1))


def dot(a, b, ca, cb):
    return lax.dot_general(a, b, (((ca,), (cb,)), ((), ())), preferred_element_type=F32)


def shift(p, by):
    return lax.rem(p + by + SIDE, SIDE)


def greet(devices):
    barrier = pltpu.get_barrier_semaphore()
    for device in devices:
        pl.semaphore_signal(barrier, inc=1, device_id=device)


def await_greetings(count):
    pl.semaphore_wait(pltpu.get_barrier_semaphore(), count)


def route_kernel(
    owners,
    blocks_ref,
    dest_ref,
    slot_ref,
    panel_hbm,
    bases_hbm,
    tiles_hbm,
    bases_out,
    cores_out,
    table_ref,
    tiles,
    panel,
    bases,
    proj,
    encoded,
    cores,
    outgoing,
    load_sem,
    own_sem,
    send_sem,
    recv_sem,
    a2a_send,
    a2a_recv,
):
    t = lax.axis_index("tile")
    x, z, c = t // 8, lax.rem(t // 2, SIDE), lax.rem(t, 2)
    count = tiles.shape[0]

    load_panel = pltpu.make_async_copy(panel_hbm, panel, load_sem.at[0])
    load_bases = pltpu.make_async_copy(bases_hbm, bases.at[x, z, c], load_sem.at[1])
    load_tiles = pltpu.make_async_copy(tiles_hbm, tiles, load_sem.at[2])
    load_bases.start()
    load_panel.start()
    load_tiles.start()

    @pl.loop(1, owners)
    def _(step):
        pl.semaphore_signal(
            pltpu.get_barrier_semaphore(),
            inc=1,
            device_id={"tile": lax.rem(t + step, owners)},
        )

    load_bases.wait()
    load_panel.wait()
    proj[x, z, c] = dot(bases[x, z, c], panel[...], 0, 0).astype(BF16)
    await_greetings(owners - 1)

    sibling = t + 1 - 2 * c
    pending = []

    class Gather:
        offsets = (None, 0, -1, 1, 2)

        def __init__(self, number, buf, x_first):
            self.n, self.buf, self.x_first = number, buf, x_first
            self.f, self.s = (x, z) if x_first else (z, x)
            self.rows = buf.shape[3]

        def at(self, first, second, core):
            return self.buf.at[(first, second, core) if self.x_first else (second, first, core)]

        def place(self, ring, by):
            if ring == 0:
                return shift(self.f, by), self.s
            return shift(self.f, self.offsets[ring]), shift(self.s, by)

        def peer(self, ring, by):
            first, second = (self.f, shift(self.s, by)) if ring else self.place(0, by)
            return (first if self.x_first else second) * 8 + (second if self.x_first else first) * 2 + c

        def copy(self, ref, peer, k):
            return pltpu.make_async_remote_copy(
                src_ref=ref,
                dst_ref=ref,
                send_sem=send_sem.at[self.n, k],
                recv_sem=recv_sem.at[self.n, k],
                device_id={"tile": peer},
            )

        def send(self, ref, peer, k):
            copy = self.copy(ref, peer, k)
            copy.start()
            pending.append(copy)

        def block(self, ring, by, half=None):
            ref = self.at(*self.place(ring, by), c)
            if half is None:
                return ref
            return ref.at[pl.ds(half * (self.rows // 2), self.rows // 2)]

        def open(self, ring):
            for k, by in enumerate((1, -1)):
                self.send(self.block(ring, 0), self.peer(ring, by), 4 * ring + k)

        def relay(self, ring):
            for k, by in enumerate((-1, 1)):
                self.copy(self.block(ring, by), self.peer(ring, by), 4 * ring + k).wait_recv()
                self.send(self.block(ring, by, k), self.peer(ring, -by), 4 * ring + 2 + k)
                if ring == 0:
                    self.open(2 + k)

        def close(self, ring):
            for k, by in enumerate((-1, 1)):
                self.copy(self.block(ring, 2, k), self.peer(ring, by), 4 * ring + 2 + k).wait_recv()
            if ring == 0:
                self.open(4)
            else:
                self.send(self.line(ring, c), sibling, 19 + ring)

        def line(self, ring, core):
            return self.at(self.place(ring, 0)[0], slice(None), core)

        def from_sibling(self, ring):
            self.copy(self.line(ring, 1 - c), sibling, 19 + ring).wait_recv()

    def of(buf, which, tile):
        block = blocks_ref[which, tile]
        return buf[block >> 3, (block >> 1) & 3, block & 1]

    def encode(start, stop):
        @pl.loop(start, stop, unroll=4)
        def _(q):
            tile = t * count + q
            half = dot(of(bases, 0, tile), tiles[q], 0, 0).astype(BF16)
            encoded[q] = dot(half, of(bases, 1, tile), 1, 0)

    both = (Gather(0, bases, True), Gather(1, proj, False))
    for step, ring in (
        ("open", 0), ("open", 1), ("relay", 0), ("relay", 1), ("close", 0), ("relay", 2),
        ("relay", 3), ("close", 1), ("relay", 4), ("close", 2), ("close", 3), ("close", 4),
        ("from_sibling", 1), ("from_sibling", 2), ("from_sibling", 3), ("from_sibling", 4),
    ):
        for gather in both:
            getattr(gather, step)(ring)
    keep_bases = pltpu.make_async_copy(bases, bases_out, own_sem.at[1])
    keep_bases.start()
    load_tiles.wait()
    encode(0, count)

    @pl.loop(0, count, unroll=4)
    def _(q):
        tile = t * count + q
        cross = dot(of(proj, 0, tile), of(proj, 1, tile), 1, 1)
        cores[q] = (encoded[q] - cross).astype(BF16)

    dests = [dest_ref[t * count + q] for q in range(count)]

    def partner(step, sign):
        off = lax.rem(step * 11, owners)
        dx, dz, dc = off // 8, lax.rem(off // 2, SIDE), lax.rem(off, 2)
        px, pz, pc = shift(x, sign * dx), shift(z, sign * dz), lax.rem(c + dc, 2)
        return px * 8 + pz * 2 + pc

    def outbound(step, source, target):
        return pltpu.make_async_remote_copy(
            src_ref=outgoing.at[step],
            dst_ref=cores_out.at[source],
            send_sem=a2a_send.at[step],
            recv_sem=a2a_recv.at[step],
            device_id={"tile": target},
        )

    def pack(step, target):
        first, last = jnp.int32(0), jnp.int32(0)
        for q in range(count):
            last = jnp.where(dests[q] == target, q, last)
            back = count - 1 - q
            first = jnp.where(dests[back] == target, back, first)
        outgoing[step, 0] = cores[first]
        outgoing[step, 1] = cores[last]

    @pl.loop(1, owners)
    def _(step):
        target = partner(step, 1)
        pack(step, target)
        outbound(step, t, target).start()

    pack(0, t)
    keep_own = pltpu.make_async_copy(outgoing.at[0], cores_out.at[t], own_sem.at[0])
    keep_own.start()

    @pl.loop(0, owners)
    def _(source):
        first, last, found = jnp.int32(0), jnp.int32(0), jnp.int32(0)
        for q in range(count):
            tile = source * count + q
            hit = dest_ref[tile] == t
            last = jnp.where(hit, tile, last)
            first = jnp.where(hit & (found == 0), tile, first)
            found = found + hit.astype(jnp.int32)
        for k, tile in enumerate((first, last)):
            entry = blocks_ref[0, tile] + blocks_ref[1, tile] * 256 + slot_ref[tile] * 65536
            table_ref[source * CAP + k] = jnp.where(found > k, entry, -1)

    @pl.loop(1, owners)
    def _(step):
        source = partner(step, -1)
        outbound(step, source, source).wait()

    keep_own.wait()
    keep_bases.wait()
    for copy in pending:
        copy.wait_send()


def decode_kernel(
    table_ref,
    pblocks_ref,
    bases_hbm,
    cores_hbm,
    parents_hbm,
    test_hbm,
    updated_hbm,
    sketch,
    bases,
    cores,
    parents,
    test,
    total,
    part,
    number_of,
    listed,
    load_sem,
    tile_sem,
    store_sem,
):
    held = parents.shape[0]
    blocks, places = part.shape[0], cores.shape[0]
    rank = cores.shape[1]

    def load(p):
        return pltpu.make_async_copy(parents_hbm.at[p], parents.at[p], tile_sem.at[p])

    def store(p):
        return pltpu.make_async_copy(parents.at[p], updated_hbm.at[p], store_sem.at[p])

    load_cores = pltpu.make_async_copy(cores_hbm, cores, load_sem.at[0])
    load_bases = pltpu.make_async_copy(bases_hbm, bases, load_sem.at[1])
    load_test = pltpu.make_async_copy(test_hbm, test, load_sem.at[2])
    load_cores.start()
    load_bases.start()
    for p in range(held):
        load(p).start()
    load_test.start()

    @pl.loop(0, blocks)
    def _(b):
        part[b] = jnp.zeros_like(part[b])

    for p in range(held):
        number_of[p] = 0

    @pl.loop(0, places)
    def _(k):
        entry = table_ref[k]

        @pl.when(entry >= 0)
        def _():
            slot = entry >> 16
            n = number_of[slot]
            listed[slot * places + n] = k
            number_of[slot] = n + 1

    empty = jnp.zeros((rank, rank), BF16)
    load_cores.wait()
    load_bases.wait()
    load_test.wait()

    @pl.loop(0, held)
    def _(p):
        load(p).wait()
        total[...] = parents[p].astype(F32)
        n = number_of[p]

        def add(at, wide):
            lefts, rights = [], []
            for pair in range(0, wide, 2):
                rows, cols, middle = [], [], []
                for one in (at + pair, at + pair + 1):
                    k = listed[p * places + jnp.minimum(one, n - 1)]
                    entry = table_ref[k]
                    rows.append(bases[entry & 255])
                    cols.append(bases[(entry >> 8) & 255])
                    middle.append(jnp.where(one < n, cores[k], empty))
                block = jnp.concatenate(
                    [
                        jnp.concatenate([middle[0], empty], axis=1),
                        jnp.concatenate([empty, middle[1]], axis=1),
                    ],
                    axis=0,
                )
                left = dot(jnp.concatenate(rows, axis=1), block, 1, 0)
                lefts.append(left.astype(BF16))
                rights += cols
            left = jnp.concatenate(lefts, axis=1)
            total[...] += dot(left, jnp.concatenate(rights, axis=1), 1, 1)

        fours = (n + 1) // 4

        @pl.loop(0, fours)
        def _(m):
            add(4 * m, 4)

        @pl.when(4 * fours < n)
        def _():
            add(4 * fours, 2)

        new = total[...].astype(BF16)
        parents[p] = new
        store(p).start()
        a, b = pblocks_ref[0, p], pblocks_ref[1, p]
        part[a] += dot(new, test[b], 1, 0)

        @pl.when(a != b)
        def _():
            part[b] += dot(new, test[a], 0, 0)

    @pl.loop(0, blocks)
    def _(b):
        sketch[b] = part[b].astype(BF16)

    for p in range(held):
        store(p).wait()


def reduce_kernel(part, out_ref, *scratch):
    n = len(SPLIT)
    heard, held, got1, held2, got2, held3, got3 = (
        scratch[i * n : (i + 1) * n] for i in range(7)
    )
    send_sem, recv_sem = scratch[7 * n :]
    y, t = lax.axis_index("child"), lax.axis_index("tile")
    x, z, c = t // 8, lax.rem(t // 2, SIDE), lax.rem(t, 2)
    here = (y, x, z)

    def device(coords, core):
        return {"child": coords[0], "tile": coords[1] * 8 + coords[2] * 2 + core}

    def moved(axis, by):
        return tuple(shift(p, by) if a == axis else p for a, p in enumerate(here))

    sibling = device(here, 1 - c)
    greet([sibling] + [device(moved(a, by), c) for a in range(3) for by in (1, 2, 3)])

    await_greetings(10)

    pending = []

    def remote(src, dst, number, peer):
        copy = pltpu.make_async_remote_copy(
            src_ref=src,
            dst_ref=dst,
            send_sem=send_sem.at[number],
            recv_sem=recv_sem.at[number],
            device_id=peer,
        )
        pending.append(copy)
        copy.start()
        return copy

    swaps = [
        remote(part.at[:, :, :, 1 - c, pl.ds(at, rows)], heard[k], 30 + k, sibling)
        for k, (at, rows) in enumerate(SPLIT)
    ]

    def pick(ref, axis, which):
        return ref.at[(slice(None),) * axis + (which,)]

    def left_axes(k, stage):
        axes = [a for a in range(3) if a not in ORDERS[k][:stage]]
        return axes.index(ORDERS[k][stage])

    def scatter(k, stage, buf, got):
        axis, copies = ORDERS[k][stage], []
        at = left_axes(k, stage)
        for by in (1, 3, 2):
            copies.append(
                remote(
                    pick(buf, at, shift(here[axis], by)),
                    got.at[by - 1],
                    9 * k + 3 * stage + by - 1,
                    device(moved(axis, by), c),
                )
            )
        return copies

    def gather_up(k, stage, buf, got, copies, dst):
        axis = ORDERS[k][stage]
        for copy in copies:
            copy.wait_recv()
        kept = pick(buf, left_axes(k, stage), here[axis])[...].astype(F32)
        value = kept + got[0].astype(F32) + got[1].astype(F32) + got[2].astype(F32)
        dst[...] = value.astype(dst.dtype)

    flying = []
    for k, (at, rows) in enumerate(SPLIT):
        swaps[k].wait_recv()

        @pl.loop(0, SIDE)
        def _(a):
            mine = part[a, :, :, c, pl.ds(at, rows)].astype(F32)
            held[k][a] = (mine + heard[k][a].astype(F32)).astype(BF16)

        flying.append(scatter(k, 0, held[k], got1[k]))
    for k in range(n):
        gather_up(k, 0, held[k], got1[k], flying[k], held2[k])
        flying[k] = scatter(k, 1, held2[k], got2[k])
    for k in range(n):
        gather_up(k, 1, held2[k], got2[k], flying[k], held3[k])
        flying[k] = scatter(k, 2, held3[k], got3[k])
    for k, (at, rows) in enumerate(SPLIT):
        gather_up(k, 2, held3[k], got3[k], flying[k], out_ref.at[pl.ds(at, rows)])
    for copy in pending:
        copy.wait_send()


def shards(
    child_tiles,
    panel,
    bases,
    tile_blocks,
    tile_dest,
    tile_slot,
    parent_tiles,
    parent_blocks,
    sketch_test,
):
    owners = lax.axis_size("tile")
    _, count, order, _ = child_tiles.shape
    rank = bases.shape[2]
    width = sketch_test.shape[1]
    held = parent_tiles.shape[1]
    blocks = sketch_test.shape[0] // order
    chunk = sketch_test.shape[0] // (SIDE**3 * 2)
    hbm = pl.BlockSpec(memory_space=pltpu.HBM)
    smem = pl.BlockSpec(memory_space=pltpu.SMEM)
    vmem = pl.BlockSpec(memory_space=pltpu.VMEM)
    dma = pltpu.SemaphoreType.DMA

    whole_bases, cores, table = pl.pallas_call(
        functools.partial(route_kernel, owners),
        out_shape=(
            jax.ShapeDtypeStruct((SIDE, SIDE, 2, order, rank), BF16),
            jax.ShapeDtypeStruct((owners, CAP, rank, rank), BF16),
            jax.ShapeDtypeStruct((owners * CAP,), jnp.int32),
        ),
        in_specs=[smem, smem, smem, hbm, hbm, hbm],
        out_specs=(hbm, hbm, smem),
        scratch_shapes=[
            pltpu.VMEM((count, order, order), BF16),
            pltpu.VMEM((order, order), BF16),
            pltpu.VMEM((SIDE, SIDE, 2, order, rank), BF16),
            pltpu.VMEM((SIDE, SIDE, 2, rank, order), BF16),
            pltpu.VMEM((count, rank, rank), F32),
            pltpu.VMEM((count, rank, rank), BF16),
            pltpu.VMEM((owners, CAP, rank, rank), BF16),
            dma((3,)),
            dma((2,)),
            dma((2, 24)),
            dma((2, 24)),
            dma((owners,)),
            dma((owners,)),
        ],
        compiler_params=pltpu.CompilerParams(
            collective_id=0, has_side_effects=True, vmem_limit_bytes=54 << 20
        ),
        name="encode_and_route",
    )(tile_blocks[0].T, tile_dest[0, :, 0], tile_slot[0], panel[0], bases[0], child_tiles[0])

    updated, part = pl.pallas_call(
        decode_kernel,
        out_shape=(
            jax.ShapeDtypeStruct((held, order, order), BF16),
            jax.ShapeDtypeStruct((blocks, order, width), BF16),
        ),
        in_specs=[smem, smem, hbm, hbm, hbm, hbm],
        out_specs=(hbm, vmem),
        scratch_shapes=[
            pltpu.VMEM((owners, order, rank), BF16),
            pltpu.VMEM((owners * CAP, rank, rank), BF16),
            pltpu.VMEM((held, order, order), BF16),
            pltpu.VMEM((blocks, order, width), BF16),
            pltpu.VMEM((order, order), F32),
            pltpu.VMEM((blocks, order, width), F32),
            pltpu.SMEM((held,), jnp.int32),
            pltpu.SMEM((held * owners * CAP,), jnp.int32),
            dma((3,)),
            dma((held,)),
            dma((held,)),
        ],
        compiler_params=pltpu.CompilerParams(vmem_limit_bytes=34 << 20),
        name="decode_and_sketch",
    )(
        table,
        parent_blocks[0].T,
        whole_bases.reshape(owners, order, rank),
        cores.reshape(owners * CAP, rank, rank),
        parent_tiles[0],
        sketch_test.reshape(blocks, order, width),
    )

    def bufs(*lead):
        return [pltpu.VMEM((*lead, rows, width), BF16) for _, rows in SPLIT]

    row_sketch = pl.pallas_call(
        reduce_kernel,
        out_shape=jax.ShapeDtypeStruct((chunk, width), F32),
        in_specs=[vmem],
        out_specs=vmem,
        scratch_shapes=[
            *bufs(4, 4, 4),
            *bufs(4, 4, 4),
            *bufs(3, 4, 4),
            *bufs(4, 4),
            *bufs(3, 4),
            *bufs(4),
            *bufs(3),
            dma((33,)),
            dma((33,)),
        ],
        compiler_params=pltpu.CompilerParams(
            collective_id=1, has_side_effects=True, vmem_limit_bytes=32 << 20
        ),
        name="reduce_sketch",
    )(part.reshape(SIDE, SIDE, SIDE, 2, chunk, width))
    return (updated[None], row_sketch)


def solution(mesh):
    return jax.shard_map(
        shards,
        mesh=mesh,
        in_specs=(
            P("child", "tile", None, None),
            P("child", "tile", None),
            P("child", "tile", None),
            P("child", None, None),
            P("child", None, None),
            P("child", None),
            P("child", "tile", None, None),
            P("child", "tile", None),
            P(),
        ),
        out_specs=(P("child", "tile", None, None), P(("child", "tile"), None)),
        check_vma=False,
    )
```

time: 154 us -> 118 us (0.77)
  Pallas kernels: 142 us -> 111 us
  local copies, waits for them, and re-layouts: 8.89 us -> 4.99 us
  other arithmetic: 2.14 us -> 0 us
    pallas_call x1, Pallas kernels: 51 us -> 31.2 us  [shards(): pl.pallas_call(reduce_kernel, out_shape=jax.ShapeDtypeStruct((chunk, widt...]
    pallas_call x1, Pallas kernels: 73.3 us -> 67.3 us  [shards(): pl.pallas_call(functools.partial(route_kernel, owners), out_shape=(jax.Sh...]
    pallas_call x1, Pallas kernels: 17.2 us -> 12.2 us  [shards(): pl.pallas_call(decode_kernel, out_shape=(jax.ShapeDtypeStruct((held, orde...]
    unnamed x12 -> x13, local copies, waits for them, and re-layouts: 8.81 us -> 4.99 us
where the time goes in v2:
time: 118 us; the launch traced here: 116 us
  Pallas kernels  111 us (94%)
  local copies, waits for them, and re-layouts  4.99 us (4%)
    pallas_call x1, Pallas kernels, shards(): pl.pallas_call(functools.partial(route_kernel, owners), out_shape=(jax.Sh...  67.3 us
    pallas_call x1, Pallas kernels, shards(): pl.pallas_call(reduce_kernel, out_shape=jax.ShapeDtypeStruct((chunk, widt...  31.2 us
    pallas_call x1, Pallas kernels, shards(): pl.pallas_call(decode_kernel, out_shape=(jax.ShapeDtypeStruct((held, orde...  12.2 us
    unnamed x13, local copies, waits for them, and re-layouts  4.99 us

profile of v2, /device:TPU:0, one launch (start us, length us, event | category | flops | bytes accessed | tf_op | source)
XLA Modules:
  0.0 116.4 jit_solution(8872871006758686841)
XLA Ops:
  0.6 0.0 copy-start
  0.6 0.0 copy-start.1
  0.7 0.0 copy-start.4
  0.7 67.3 %encode_and_route.1 = (bf16[4,4,2,512,128]{4,3,2,1,0:T(8,128)(2,1)}, bf16[32,2,128,128]{3,2,1,0:T(8,128)(2,1)}, s32[64]{0:T(128)}) custom-call(s32[2,512]{1,0:T(2,128)} %bitcast.26, s32[512]{0:T(512)} %bitcast.27, s32[512]{0:T(512)} %bitcast.28, bf16[512,512]{1,0:T(8,128)(2,1)} %bitcast.24, bf16[512,128]{1,0:T(8,128)(2,1)} %bitcast.25, ...), custom_call_target="tpu_custom_call" | custom-call | tf_op jit(solution)/shard_map/encode_and_route/pallas_call | solution.py:477
  67.9 0.0 copy-done
  67.9 0.0 copy-done.1
  68.0 0.0 copy-done.4
  68.0 0.0 copy-start.2
  68.0 2.2 %copy-done.2 = bf16[4,4,2,512,128]{4,3,2,1,0:T(8,128)(2,1)S(1)} copy-done((bf16[4,4,2,512,128]{4,3,2,1,0:T(8,128)(2,1)S(1)}, bf16[4,4,2,512,128]{4,3,2,1,0:T(8,128)(2,1)}, u32[]{:S(2)}) %copy-start.2) | copy-done | bytes 4194328
  70.2 0.0 copy-start.3
  70.2 1.6 %copy-done.3 = bf16[32,2,128,128]{3,2,1,0:T(8,128)(2,1)S(1)} copy-done((bf16[32,2,128,128]{3,2,1,0:T(8,128)(2,1)S(1)}, bf16[32,2,128,128]{3,2,1,0:T(8,128)(2,1)}, u32[]{:S(2)}) %copy-start.3) | copy-done | bytes 2097176
  71.7 0.0 copy-start.5
  71.8 0.6 copy-done.5
  72.3 12.2 %decode_and_sketch.1 = (bf16[8,512,512]{2,1,0:T(8,128)(2,1)}, bf16[32,512,128]{2,1,0:T(8,128)(2,1)S(1)}) custom-call(s32[64]{0:T(128)S(1)} %copy-done.5, s32[2,8]{1,0:T(2,128)S(1)} %bitcast.22, bf16[32,512,128]{2,1,0:T(8,128)(2,1)S(1)} %bitcast.19, bf16[64,128,128]{2,1,0:T(8,128)(2,1)S(1)} %bitcast.21, bf16[8,512,512]{2,1,0:T(8,128)(2,1)S(1)} %bitcast.17, ...), custom_call_target="tpu_custom_call" | custom-call | tf_op jit(solution)/shard_map/decode_and_sketch/pallas_call | solution.py:507
  84.6 31.2 %reduce_sketch.1 = f32[128,128]{1,0:T(8,128)S(1)} custom-call(bf16[4,4,4,2,128,128]{5,4,3,2,1,0:T(8,128)(2,1)S(1)} %bitcast.20), custom_call_target="tpu_custom_call" | custom-call | tf_op jit(solution)/shard_map/reduce_sketch/pallas_call | solution.py:542
  115.8 0.6 copy.12
Async XLA Ops:
  0.6 67.3 %copy-start = (bf16[1,8,512,512]{3,2,1,0:T(8,128)(2,1)S(1)}, bf16[1,8,512,512]{3,2,1,0:T(8,128)(2,1)}, u32[]{:S(2)}) copy-start(bf16[1,8,512,512]{3,2,1,0:T(8,128)(2,1)} %param.15) | copy-start | bytes 12582916
  0.6 67.3 %copy-start.1 = (bf16[16384,128]{1,0:T(8,128)(2,1)S(1)}, bf16[16384,128]{1,0:T(8,128)(2,1)}, u32[]{:S(2)}) copy-start(bf16[16384,128]{1,0:T(8,128)(2,1)} %param.17) | copy-start | bytes 12582916
  0.7 67.3 %copy-start.4 = (s32[1,8,2]{1,2,0:T(2,128)S(1)}, s32[1,8,2]{1,2,0:T(2,128)}, u32[]{:S(2)}) copy-start(s32[1,8,2]{1,2,0:T(2,128)} %param.16) | copy-start | bytes 196
  68.0 2.2 %copy-start.2 = (bf16[4,4,2,512,128]{4,3,2,1,0:T(8,128)(2,1)S(1)}, bf16[4,4,2,512,128]{4,3,2,1,0:T(8,128)(2,1)}, u32[]{:S(2)}) copy-start(bf16[4,4,2,512,128]{4,3,2,1,0:T(8,128)(2,1)} %get-tuple-element.8) | copy-start | bytes 12582916
  70.2 1.6 %copy-start.3 = (bf16[32,2,128,128]{3,2,1,0:T(8,128)(2,1)S(1)}, bf16[32,2,128,128]{3,2,1,0:T(8,128)(2,1)}, u32[]{:S(2)}) copy-start(bf16[32,2,128,128]{3,2,1,0:T(8,128)(2,1)} %get-tuple-element.9) | copy-start | bytes 6291460
  71.7 0.6 copy-start.5

commit v3 on v2

--- a/solution.py
+++ b/solution.py
@@ -11,6 +11,13 @@
 SIDE = 4
 F32 = jnp.float32
 BF16 = jnp.bfloat16
+PLAN = (
+    (0, 0), (0, 1), (5, 0), (0, 2), (0, 3), (0, 4), (0, 5), (0, 6), (1, 0), (1, 1), (0, 7), (0, 8),
+    (0, 9), (0, 10), (0, 11), (1, 2), (1, 3), (0, 12), (0, 13), (0, 14), (0, 15), (1, 4),
+    (2, 0), (1, 5), (2, 1), (1, 6), (2, 2), (1, 7), (2, 3), (1, 8),
+    (3, 0), (1, 9), (3, 1), (1, 10), (3, 2), (1, 11), (3, 3), (4, 0), (1, 12), (1, 13), (1, 14), (1, 15),
+)
+SHARED = 40
 SPLIT = ((0, 48), (48, 48), (96, 32))
 ORDERS = ((0, 1, 2), (1, 2, 0), (2, 0, 1))
 
@@ -41,18 +48,19 @@
     panel_hbm,
     bases_hbm,
     tiles_hbm,
-    bases_out,
-    cores_out,
+    shared,
     table_ref,
     tiles,
     panel,
     bases,
     proj,
-    encoded,
     cores,
     outgoing,
+    incoming,
+    settled,
     load_sem,
     own_sem,
+    keep_sem,
     send_sem,
     recv_sem,
     a2a_send,
@@ -60,7 +68,7 @@
 ):
     t = lax.axis_index("tile")
     x, z, c = t // 8, lax.rem(t // 2, SIDE), lax.rem(t, 2)
-    count = tiles.shape[0]
+    count, rank = tiles.shape[0], cores.shape[1]
 
     load_panel = pltpu.make_async_copy(panel_hbm, panel, load_sem.at[0])
     load_bases = pltpu.make_async_copy(bases_hbm, bases.at[x, z, c], load_sem.at[1])
@@ -78,8 +86,6 @@
         )
 
     load_bases.wait()
-    load_panel.wait()
-    proj[x, z, c] = dot(bases[x, z, c], panel[...], 0, 0).astype(BF16)
     await_greetings(owners - 1)
 
     sibling = t + 1 - 2 * c
@@ -91,10 +97,12 @@
         def __init__(self, number, buf, x_first):
             self.n, self.buf, self.x_first = number, buf, x_first
             self.f, self.s = (x, z) if x_first else (z, x)
-            self.rows = buf.shape[3]
-
-        def at(self, first, second, core):
-            return self.buf.at[(first, second, core) if self.x_first else (second, first, core)]
+            self.rows = buf.shape[3] // 2
+            self.start = 0 if x_first else self.rows
+
+        def at(self, first, second, core, at=0, rows=None):
+            place = (first, second) if self.x_first else (second, first)
+            return self.buf.at[(*place, core, pl.ds(self.start + at, rows or self.rows))]
 
         def place(self, ring, by):
             if ring == 0:
@@ -120,29 +128,30 @@
             pending.append(copy)
 
         def block(self, ring, by, half=None):
-            ref = self.at(*self.place(ring, by), c)
             if half is None:
-                return ref
-            return ref.at[pl.ds(half * (self.rows // 2), self.rows // 2)]
+                return self.at(*self.place(ring, by), c)
+            return self.at(*self.place(ring, by), c, half * (self.rows // 2), self.rows // 2)
 
         def open(self, ring):
-            for k, by in enumerate((1, -1)):
+            for k, by in enumerate((1, -1) if ring else (1, -1, 2)):
                 self.send(self.block(ring, 0), self.peer(ring, by), 4 * ring + k)
 
         def relay(self, ring):
             for k, by in enumerate((-1, 1)):
                 self.copy(self.block(ring, by), self.peer(ring, by), 4 * ring + k).wait_recv()
-                self.send(self.block(ring, by, k), self.peer(ring, -by), 4 * ring + 2 + k)
-                if ring == 0:
+                if ring:
+                    self.send(self.block(ring, by, k), self.peer(ring, -by), 4 * ring + 2 + k)
+                else:
                     self.open(2 + k)
 
         def close(self, ring):
+            if ring == 0:
+                self.copy(self.block(0, 2), self.peer(0, 2), 2).wait_recv()
+                self.open(4)
+                return
             for k, by in enumerate((-1, 1)):
                 self.copy(self.block(ring, 2, k), self.peer(ring, by), 4 * ring + 2 + k).wait_recv()
-            if ring == 0:
-                self.open(4)
-            else:
-                self.send(self.line(ring, c), sibling, 19 + ring)
+            self.send(self.line(ring, c), sibling, 19 + ring)
 
         def line(self, ring, core):
             return self.at(self.place(ring, 0)[0], slice(None), core)
@@ -159,27 +168,17 @@
         def _(q):
             tile = t * count + q
             half = dot(of(bases, 0, tile), tiles[q], 0, 0).astype(BF16)
-            encoded[q] = dot(half, of(bases, 1, tile), 1, 0)
-
-    both = (Gather(0, bases, True), Gather(1, proj, False))
-    for step, ring in (
+            cores[q] = dot(half, of(bases, 1, tile), 1, 0).astype(BF16)
+
+    steps = (
         ("open", 0), ("open", 1), ("relay", 0), ("relay", 1), ("close", 0), ("relay", 2),
         ("relay", 3), ("close", 1), ("relay", 4), ("close", 2), ("close", 3), ("close", 4),
         ("from_sibling", 1), ("from_sibling", 2), ("from_sibling", 3), ("from_sibling", 4),
-    ):
-        for gather in both:
-            getattr(gather, step)(ring)
-    keep_bases = pltpu.make_async_copy(bases, bases_out, own_sem.at[1])
-    keep_bases.start()
-    load_tiles.wait()
-    encode(0, count)
-
-    @pl.loop(0, count, unroll=4)
-    def _(q):
-        tile = t * count + q
-        cross = dot(of(proj, 0, tile), of(proj, 1, tile), 1, 1)
-        cores[q] = (encoded[q] - cross).astype(BF16)
-
+    )
+    arrays = (
+        (Gather(0, bases, True), Gather(1, bases, False)),
+        (Gather(2, proj, True), Gather(3, proj, False)),
+    )
     dests = [dest_ref[t * count + q] for q in range(count)]
 
     def partner(step, sign):
@@ -191,7 +190,7 @@
     def outbound(step, source, target):
         return pltpu.make_async_remote_copy(
             src_ref=outgoing.at[step],
-            dst_ref=cores_out.at[source],
+            dst_ref=incoming.at[source],
             send_sem=a2a_send.at[step],
             recv_sem=a2a_recv.at[step],
             device_id={"tile": target},
@@ -206,35 +205,80 @@
         outgoing[step, 0] = cores[first]
         outgoing[step, 1] = cores[last]
 
-    @pl.loop(1, owners)
-    def _(step):
-        target = partner(step, 1)
-        pack(step, target)
-        outbound(step, t, target).start()
+    def dispatch(start, stop):
+        @pl.loop(max(start, 1), stop)
+        def _(step):
+            target = partner(step, 1)
+            pack(step, target)
+            outbound(step, t, target).start()
+
+    def foretell():
+        @pl.loop(0, owners)
+        def _(source):
+            first, last, found = jnp.int32(0), jnp.int32(0), jnp.int32(0)
+            for q in range(count):
+                tile = source * count + q
+                hit = dest_ref[tile] == t
+                last = jnp.where(hit, tile, last)
+                first = jnp.where(hit & (found == 0), tile, first)
+                found = found + hit.astype(jnp.int32)
+            for k, tile in enumerate((first, last)):
+                entry = blocks_ref[0, tile] + blocks_ref[1, tile] * 256 + slot_ref[tile] * 65536
+                table_ref[source * CAP + k] = jnp.where(found > k, entry, -1)
+
+    each, wave = count // 4, owners // 4
+    for what, at in PLAN:
+        if what == 2:
+            if at == 0:
+                keep_bases = pltpu.make_async_copy(bases, shared.at[pl.ds(0, SIDE)], own_sem.at[1])
+                keep_bases.start()
+                load_tiles.wait()
+            encode(at * each, at * each + each)
+        elif what == 3:
+            dispatch(at * wave, at * wave + wave)
+        elif what == 4:
+            foretell()
+        elif what == 5:
+            load_panel.wait()
+            proj[x, z, c] = dot(bases[x, z, c], panel[...], 0, 0).astype(BF16)
+        else:
+            step, ring = steps[at]
+            for gather in arrays[what]:
+                getattr(gather, step)(ring)
+
+    def keep(source):
+        place = (source // 16, lax.rem(source // 4, SIDE), lax.rem(source // 2, 2))
+        rows = pl.ds(pl.multiple_of(lax.rem(source, 2) * CAP * rank, CAP * rank), CAP * rank)
+        return pltpu.make_async_copy(
+            settled.at[source],
+            shared.at[SIDE + place[0], place[1], place[2], rows],
+            keep_sem.at[source],
+        )
+
+    def settle(source, received):
+        for k in range(CAP):
+            entry = jnp.maximum(table_ref[source * CAP + k], 0)
+            i, j = entry & 255, (entry >> 8) & 255
+            cross = dot(
+                proj[i >> 3, (i >> 1) & 3, i & 1], proj[j >> 3, (j >> 1) & 3, j & 1], 1, 1
+            )
+            core = received[k].astype(F32) - cross
+            settled[source, k * rank : (k + 1) * rank] = core.astype(BF16)
+        keep(source).start()
 
     pack(0, t)
-    keep_own = pltpu.make_async_copy(outgoing.at[0], cores_out.at[t], own_sem.at[0])
-    keep_own.start()
-
-    @pl.loop(0, owners)
-    def _(source):
-        first, last, found = jnp.int32(0), jnp.int32(0), jnp.int32(0)
-        for q in range(count):
-            tile = source * count + q
-            hit = dest_ref[tile] == t
-            last = jnp.where(hit, tile, last)
-            first = jnp.where(hit & (found == 0), tile, first)
-            found = found + hit.astype(jnp.int32)
-        for k, tile in enumerate((first, last)):
-            entry = blocks_ref[0, tile] + blocks_ref[1, tile] * 256 + slot_ref[tile] * 65536
-            table_ref[source * CAP + k] = jnp.where(found > k, entry, -1)
+    settle(t, outgoing.at[0])
 
     @pl.loop(1, owners)
     def _(step):
         source = partner(step, -1)
         outbound(step, source, source).wait()
-
-    keep_own.wait()
+        settle(source, incoming.at[source])
+
+    @pl.loop(0, owners)
+    def _(source):
+        keep(source).wait()
+
     keep_bases.wait()
     for copy in pending:
         copy.wait_send()
@@ -243,8 +287,7 @@
 def decode_kernel(
     table_ref,
     pblocks_ref,
-    bases_hbm,
-    cores_hbm,
+    shared,
     parents_hbm,
     test_hbm,
     updated_hbm,
@@ -262,8 +305,8 @@
     store_sem,
 ):
     held = parents.shape[0]
-    blocks, places = part.shape[0], cores.shape[0]
-    rank = cores.shape[1]
+    blocks, places = part.shape[0], table_ref.shape[0]
+    rank = cores.shape[4]
 
     def load(p):
         return pltpu.make_async_copy(parents_hbm.at[p], parents.at[p], tile_sem.at[p])
@@ -271,8 +314,8 @@
     def store(p):
         return pltpu.make_async_copy(parents.at[p], updated_hbm.at[p], store_sem.at[p])
 
-    load_cores = pltpu.make_async_copy(cores_hbm, cores, load_sem.at[0])
-    load_bases = pltpu.make_async_copy(bases_hbm, bases, load_sem.at[1])
+    load_cores = pltpu.make_async_copy(shared.at[pl.ds(SIDE, 2)], cores, load_sem.at[0])
+    load_bases = pltpu.make_async_copy(shared.at[pl.ds(0, SIDE)], bases, load_sem.at[1])
     load_test = pltpu.make_async_copy(test_hbm, test, load_sem.at[2])
     load_cores.start()
     load_bases.start()
@@ -297,6 +340,13 @@
             n = number_of[slot]
             listed[slot * places + n] = k
             number_of[slot] = n + 1
+
+    def basis(block):
+        return bases[block >> 3, (block >> 1) & 3, block & 1]
+
+    def core(k):
+        rows = pl.ds(pl.multiple_of((k & 3) * rank, rank), rank)
+        return cores[k >> 5, (k >> 3) & 3, (k >> 2) & 1, rows]
 
     empty = jnp.zeros((rank, rank), BF16)
     load_cores.wait()
@@ -316,9 +366,9 @@
                 for one in (at + pair, at + pair + 1):
                     k = listed[p * places + jnp.minimum(one, n - 1)]
                     entry = table_ref[k]
-                    rows.append(bases[entry & 255])
-                    cols.append(bases[(entry >> 8) & 255])
-                    middle.append(jnp.where(one < n, cores[k], empty))
+                    rows.append(basis(entry & 255))
+                    cols.append(basis((entry >> 8) & 255))
+                    middle.append(jnp.where(one < n, core(k), empty))
                 block = jnp.concatenate(
                     [
                         jnp.concatenate([middle[0], empty], axis=1),
@@ -474,27 +524,28 @@
     vmem = pl.BlockSpec(memory_space=pltpu.VMEM)
     dma = pltpu.SemaphoreType.DMA
 
-    whole_bases, cores, table = pl.pallas_call(
+    shared, table = pl.pallas_call(
         functools.partial(route_kernel, owners),
         out_shape=(
-            jax.ShapeDtypeStruct((SIDE, SIDE, 2, order, rank), BF16),
-            jax.ShapeDtypeStruct((owners, CAP, rank, rank), BF16),
+            jax.ShapeDtypeStruct((SHARED, SIDE, 2, order, rank), BF16),
             jax.ShapeDtypeStruct((owners * CAP,), jnp.int32),
         ),
         in_specs=[smem, smem, smem, hbm, hbm, hbm],
-        out_specs=(hbm, hbm, smem),
+        out_specs=(hbm, smem),
         scratch_shapes=[
             pltpu.VMEM((count, order, order), BF16),
             pltpu.VMEM((order, order), BF16),
             pltpu.VMEM((SIDE, SIDE, 2, order, rank), BF16),
             pltpu.VMEM((SIDE, SIDE, 2, rank, order), BF16),
-            pltpu.VMEM((count, rank, rank), F32),
             pltpu.VMEM((count, rank, rank), BF16),
             pltpu.VMEM((owners, CAP, rank, rank), BF16),
+            pltpu.VMEM((owners, CAP, rank, rank), BF16),
+            pltpu.VMEM((owners, CAP * rank, rank), BF16),
             dma((3,)),
             dma((2,)),
-            dma((2, 24)),
-            dma((2, 24)),
+            dma((owners,)),
+            dma((4, 24)),
+            dma((4, 24)),
             dma((owners,)),
             dma((owners,)),
         ],
@@ -510,11 +561,11 @@
             jax.ShapeDtypeStruct((held, order, order), BF16),
             jax.ShapeDtypeStruct((blocks, order, width), BF16),
         ),
-        in_specs=[smem, smem, hbm, hbm, hbm, hbm],
+        in_specs=[smem, smem, hbm, hbm, hbm],
         out_specs=(hbm, vmem),
         scratch_shapes=[
-            pltpu.VMEM((owners, order, rank), BF16),
-            pltpu.VMEM((owners * CAP, rank, rank), BF16),
+            pltpu.VMEM((SIDE, SIDE, 2, order, rank), BF16),
+            pltpu.VMEM((2, SIDE, 2, order, rank), BF16),
             pltpu.VMEM((held, order, order), BF16),
             pltpu.VMEM((blocks, order, width), BF16),
             pltpu.VMEM((order, order), F32),
@@ -530,8 +581,7 @@
     )(
         table,
         parent_blocks[0].T,
-        whole_bases.reshape(owners, order, rank),
-        cores.reshape(owners * CAP, rank, rank),
+        shared,
         parent_tiles[0],
         sketch_test.reshape(blocks, order, width),
     )

time: 118 us -> 112 us (0.949)
  local copies, waits for them, and re-layouts: 4.99 us -> 1.3 us
  Pallas kernels: 111 us -> 109 us
    pallas_call x1, Pallas kernels: 67.3 us -> 63.1 us  [shards(): pl.pallas_call(functools.partial(route_kernel, owners), out_shape=(jax.Sh...]
    unnamed x13 -> x9, local copies, waits for them, and re-layouts: 4.99 us -> 1.3 us
    pallas_call x1, Pallas kernels: 31.2 us -> 33.6 us  [shards(): pl.pallas_call(reduce_kernel, out_shape=jax.ShapeDtypeStruct((chunk, widt...]
where the time goes in v3:
time: 112 us; the launch traced here: 111 us
  Pallas kernels  109 us (97%)
  local copies, waits for them, and re-layouts  1.3 us (1%)
    pallas_call x1, Pallas kernels, shards(): pl.pallas_call(functools.partial(route_kernel, owners), out_shape=(jax.Sh...  63.1 us
    pallas_call x1, Pallas kernels, shards(): pl.pallas_call(reduce_kernel, out_shape=jax.ShapeDtypeStruct((chunk, widt...  33.6 us
    pallas_call x1, Pallas kernels, shards(): pl.pallas_call(decode_kernel, out_shape=(jax.ShapeDtypeStruct((held, orde...  12.7 us

profile of v3, /device:TPU:0, one launch (start us, length us, event | category | flops | bytes accessed | tf_op | source)
XLA Modules:
  0.0 111.4 jit_solution(15643138678714981129)
XLA Ops:
  0.6 0.0 copy-start
  0.6 0.0 copy-start.1
  0.7 0.0 copy-start.2
  0.7 63.1 %encode_and_route.1 = (bf16[40,4,2,512,128]{4,3,2,1,0:T(8,128)(2,1)}, s32[64]{0:T(128)}) custom-call(s32[2,512]{1,0:T(2,128)} %bitcast.22, s32[512]{0:T(512)} %bitcast.23, s32[512]{0:T(512)} %bitcast.24, bf16[512,512]{1,0:T(8,128)(2,1)} %bitcast.20, bf16[512,128]{1,0:T(8,128)(2,1)} %bitcast.21, bf16[16,512,512]{2,1,0:T(8,128)(2,1)} %bitcast.19), custom_call_target="tpu_custom_call" | custom-call | tf_op jit(solution)/shard_map/encode_and_route/pallas_call | solution.py:527
  63.7 0.0 copy-done
  63.8 0.0 copy-done.1
  63.8 0.0 copy-done.2
  63.8 0.0 copy-start.3
  63.8 0.7 copy-done.3
  64.4 12.7 %decode_and_sketch.1 = (bf16[8,512,512]{2,1,0:T(8,128)(2,1)}, bf16[32,512,128]{2,1,0:T(8,128)(2,1)S(1)}) custom-call(s32[64]{0:T(128)S(1)} %copy-done.3, s32[2,8]{1,0:T(2,128)S(1)} %bitcast.18, bf16[40,4,2,512,128]{4,3,2,1,0:T(8,128)(2,1)} %get-tuple-element.7.shared, bf16[8,512,512]{2,1,0:T(8,128)(2,1)S(1)} %bitcast.15, bf16[32,512,128]{2,1,0:T(8,128)(2,1)S(1)} %bitcast.16), custom_call_target="tpu_custom_call" | custom-call | tf_op jit(solution)/shard_map/decode_and_sketch/pallas_call | solution.py:558
  77.1 33.6 %reduce_sketch.1 = f32[128,128]{1,0:T(8,128)S(1)} custom-call(bf16[4,4,4,2,128,128]{5,4,3,2,1,0:T(8,128)(2,1)S(1)} %bitcast.17), custom_call_target="tpu_custom_call" | custom-call | tf_op jit(solution)/shard_map/reduce_sketch/pallas_call | solution.py:592
  110.8 0.6 copy.12
Async XLA Ops:
  0.6 63.1 %copy-start = (bf16[1,8,512,512]{3,2,1,0:T(8,128)(2,1)S(1)}, bf16[1,8,512,512]{3,2,1,0:T(8,128)(2,1)}, u32[]{:S(2)}) copy-start(bf16[1,8,512,512]{3,2,1,0:T(8,128)(2,1)} %param.15) | copy-start | bytes 12582916
  0.6 63.1 %copy-start.1 = (bf16[16384,128]{1,0:T(8,128)(2,1)S(1)}, bf16[16384,128]{1,0:T(8,128)(2,1)}, u32[]{:S(2)}) copy-start(bf16[16384,128]{1,0:T(8,128)(2,1)} %param.17) | copy-start | bytes 12582916
  0.7 63.1 %copy-start.2 = (s32[1,8,2]{1,2,0:T(2,128)S(1)}, s32[1,8,2]{1,2,0:T(2,128)}, u32[]{:S(2)}) copy-start(s32[1,8,2]{1,2,0:T(2,128)} %param.16) | copy-start | bytes 196
  63.8 0.7 copy-start.3

commit v4 on v3

--- a/solution.py
+++ b/solution.py
@@ -18,8 +18,8 @@
     (3, 0), (1, 9), (3, 1), (1, 10), (3, 2), (1, 11), (3, 3), (4, 0), (1, 12), (1, 13), (1, 14), (1, 15),
 )
 SHARED = 40
-SPLIT = ((0, 48), (48, 48), (96, 32))
-ORDERS = ((0, 1, 2), (1, 2, 0), (2, 0, 1))
+SPLIT = ((0, 32), (32, 32), (64, 16), (80, 16), (96, 16), (112, 16))
+ORDERS = ((0, 1, 2), (1, 2, 0), (2, 0, 1)) * 2
 
 
 def dot(a, b, ca, cb):
@@ -382,15 +382,22 @@
             left = jnp.concatenate(lefts, axis=1)
             total[...] += dot(left, jnp.concatenate(rights, axis=1), 1, 1)
 
-        fours = (n + 1) // 4
+        eights = n // 8
+
+        @pl.loop(0, eights)
+        def _(m):
+            add(8 * m, 8)
+
+        rest = n - 8 * eights
+        fours = (rest + 1) // 4
 
         @pl.loop(0, fours)
         def _(m):
-            add(4 * m, 4)
-
-        @pl.when(4 * fours < n)
+            add(8 * eights + 4 * m, 4)
+
+        @pl.when(4 * fours < rest)
         def _():
-            add(4 * fours, 2)
+            add(8 * eights + 4 * fours, 2)
 
         new = total[...].astype(BF16)
         parents[p] = new
@@ -446,7 +453,7 @@
         return copy
 
     swaps = [
-        remote(part.at[:, :, :, 1 - c, pl.ds(at, rows)], heard[k], 30 + k, sibling)
+        remote(part.at[:, :, :, 1 - c, pl.ds(at, rows)], heard[k], 9 * n + k, sibling)
         for k, (at, rows) in enumerate(SPLIT)
     ]
 
@@ -460,7 +467,7 @@
     def scatter(k, stage, buf, got):
         axis, copies = ORDERS[k][stage], []
         at = left_axes(k, stage)
-        for by in (1, 3, 2):
+        for by in (2, 1, 3):
             copies.append(
                 remote(
                     pick(buf, at, shift(here[axis], by)),
@@ -602,8 +609,8 @@
             *bufs(3, 4),
             *bufs(4),
             *bufs(3),
-            dma((33,)),
-            dma((33,)),
+            dma((10 * len(SPLIT),)),
+            dma((10 * len(SPLIT),)),
         ],
         compiler_params=pltpu.CompilerParams(
             collective_id=1, has_side_effects=True, vmem_limit_bytes=32 << 20

time: 112 us -> 109 us (0.973)
  Pallas kernels: 109 us -> 107 us
    pallas_call x1, Pallas kernels: 33.6 us -> 31.5 us  [shards(): pl.pallas_call(reduce_kernel, out_shape=jax.ShapeDtypeStruct((chunk, widt...]
where the time goes in v4:
time: 109 us
  Pallas kernels  107 us (98%)
  local copies, waits for them, and re-layouts  1.3 us (1%)
    pallas_call x1, Pallas kernels, shards(): pl.pallas_call(functools.partial(route_kernel, owners), out_shape=(jax.Sh...  63.1 us
    pallas_call x1, Pallas kernels, shards(): pl.pallas_call(reduce_kernel, out_shape=jax.ShapeDtypeStruct((chunk, widt...  31.5 us
    pallas_call x1, Pallas kernels, shards(): pl.pallas_call(decode_kernel, out_shape=(jax.ShapeDtypeStruct((held, orde...  12.5 us

profile of v4, /device:TPU:0, one launch (start us, length us, event | category | flops | bytes accessed | tf_op | source)
XLA Modules:
  0.0 109.1 jit_solution(5040299295588812207)
XLA Ops:
  0.6 0.0 copy-start
  0.6 0.0 copy-start.1
  0.7 0.0 copy-start.2
  0.7 63.1 %encode_and_route.1 = (bf16[40,4,2,512,128]{4,3,2,1,0:T(8,128)(2,1)}, s32[64]{0:T(128)}) custom-call(s32[2,512]{1,0:T(2,128)} %bitcast.22, s32[512]{0:T(512)} %bitcast.23, s32[512]{0:T(512)} %bitcast.24, bf16[512,512]{1,0:T(8,128)(2,1)} %bitcast.20, bf16[512,128]{1,0:T(8,128)(2,1)} %bitcast.21, bf16[16,512,512]{2,1,0:T(8,128)(2,1)} %bitcast.19), custom_call_target="tpu_custom_call" | custom-call | tf_op jit(solution)/shard_map/encode_and_route/pallas_call | solution.py:534
  63.7 0.0 copy-done
  63.8 0.0 copy-done.1
  63.8 0.0 copy-done.2
  63.8 0.0 copy-start.3
  63.8 0.7 copy-done.3
  64.4 12.5 %decode_and_sketch.1 = (bf16[8,512,512]{2,1,0:T(8,128)(2,1)}, bf16[32,512,128]{2,1,0:T(8,128)(2,1)S(1)}) custom-call(s32[64]{0:T(128)S(1)} %copy-done.3, s32[2,8]{1,0:T(2,128)S(1)} %bitcast.18, bf16[40,4,2,512,128]{4,3,2,1,0:T(8,128)(2,1)} %get-tuple-element.7.shared, bf16[8,512,512]{2,1,0:T(8,128)(2,1)S(1)} %bitcast.15, bf16[32,512,128]{2,1,0:T(8,128)(2,1)S(1)} %bitcast.16), custom_call_target="tpu_custom_call" | custom-call | tf_op jit(solution)/shard_map/decode_and_sketch/pallas_call | solution.py:565
  77.0 31.5 %reduce_sketch.1 = f32[128,128]{1,0:T(8,128)S(1)} custom-call(bf16[4,4,4,2,128,128]{5,4,3,2,1,0:T(8,128)(2,1)S(1)} %bitcast.17), custom_call_target="tpu_custom_call" | custom-call | tf_op jit(solution)/shard_map/reduce_sketch/pallas_call | solution.py:599
  108.5 0.6 copy.12
Async XLA Ops:
  0.6 63.1 %copy-start = (bf16[1,8,512,512]{3,2,1,0:T(8,128)(2,1)S(1)}, bf16[1,8,512,512]{3,2,1,0:T(8,128)(2,1)}, u32[]{:S(2)}) copy-start(bf16[1,8,512,512]{3,2,1,0:T(8,128)(2,1)} %param.15) | copy-start | bytes 12582916
  0.6 63.1 %copy-start.1 = (bf16[16384,128]{1,0:T(8,128)(2,1)S(1)}, bf16[16384,128]{1,0:T(8,128)(2,1)}, u32[]{:S(2)}) copy-start(bf16[16384,128]{1,0:T(8,128)(2,1)} %param.17) | copy-start | bytes 12582916
  0.7 63.1 %copy-start.2 = (s32[1,8,2]{1,2,0:T(2,128)S(1)}, s32[1,8,2]{1,2,0:T(2,128)}, u32[]{:S(2)}) copy-start(s32[1,8,2]{1,2,0:T(2,128)} %param.16) | copy-start | bytes 196
  63.8 0.7 copy-start.3

commit v5 on v4

--- a/solution.py
+++ b/solution.py
@@ -300,6 +300,7 @@
     part,
     number_of,
     listed,
+    touched,
     load_sem,
     tile_sem,
     store_sem,
@@ -325,7 +326,8 @@
 
     @pl.loop(0, blocks)
     def _(b):
-        part[b] = jnp.zeros_like(part[b])
+        sketch[b] = jnp.zeros_like(sketch[b])
+        touched[b] = 0
 
     for p in range(held):
         number_of[p] = 0
@@ -347,6 +349,19 @@
     def core(k):
         rows = pl.ds(pl.multiple_of((k & 3) * rank, rank), rank)
         return cores[k >> 5, (k >> 3) & 3, (k >> 2) & 1, rows]
+
+    def accumulate(block, value):
+        seen = touched[block]
+
+        @pl.when(seen == 0)
+        def _():
+            part[block] = value
+
+        @pl.when(seen > 0)
+        def _():
+            part[block] += value
+
+        touched[block] = 1
 
     empty = jnp.zeros((rank, rank), BF16)
     load_cores.wait()
@@ -382,13 +397,13 @@
             left = jnp.concatenate(lefts, axis=1)
             total[...] += dot(left, jnp.concatenate(rights, axis=1), 1, 1)
 
-        eights = n // 8
+        eights = (n + 3) // 8
 
         @pl.loop(0, eights)
         def _(m):
             add(8 * m, 8)
 
-        rest = n - 8 * eights
+        rest = jnp.maximum(n - 8 * eights, 0)
         fours = (rest + 1) // 4
 
         @pl.loop(0, fours)
@@ -403,15 +418,17 @@
         parents[p] = new
         store(p).start()
         a, b = pblocks_ref[0, p], pblocks_ref[1, p]
-        part[a] += dot(new, test[b], 1, 0)
+        accumulate(a, dot(new, test[b], 1, 0))
 
         @pl.when(a != b)
         def _():
-            part[b] += dot(new, test[a], 0, 0)
+            accumulate(b, dot(new, test[a], 0, 0))
 
     @pl.loop(0, blocks)
     def _(b):
-        sketch[b] = part[b].astype(BF16)
+        @pl.when(touched[b] > 0)
+        def _():
+            sketch[b] = part[b].astype(BF16)
 
     for p in range(held):
         store(p).wait()
@@ -579,6 +596,7 @@
             pltpu.VMEM((blocks, order, width), F32),
             pltpu.SMEM((held,), jnp.int32),
             pltpu.SMEM((held * owners * CAP,), jnp.int32),
+            pltpu.SMEM((blocks,), jnp.int32),
             dma((3,)),
             dma((held,)),
             dma((held,)),

time: 109 us -> 110 us (level)
    pallas_call x1, Pallas kernels: 12.5 us -> 18.2 us  [shards(): pl.pallas_call(decode_kernel, out_shape=(jax.ShapeDtypeStruct((held, orde...]
    pallas_call x1, Pallas kernels: 31.5 us -> 26.7 us  [shards(): pl.pallas_call(reduce_kernel, out_shape=jax.ShapeDtypeStruct((chunk, widt...]
where the time goes in v5:
time: 110 us
  Pallas kernels  108 us (98%)
  local copies, waits for them, and re-layouts  1.3 us (1%)
    pallas_call x1, Pallas kernels, shards(): pl.pallas_call(functools.partial(route_kernel, owners), out_shape=(jax.Sh...  63.1 us
    pallas_call x1, Pallas kernels, shards(): pl.pallas_call(reduce_kernel, out_shape=jax.ShapeDtypeStruct((chunk, widt...  26.7 us
    pallas_call x1, Pallas kernels, shards(): pl.pallas_call(decode_kernel, out_shape=(jax.ShapeDtypeStruct((held, orde...  18.2 us

profile of v5, /device:TPU:0, one launch (start us, length us, event | category | flops | bytes accessed | tf_op | source)
XLA Modules:
  0.0 110.0 jit_solution(10972110247763736650)
XLA Ops:
  0.6 0.0 copy-start
  0.6 0.0 copy-start.1
  0.7 0.0 copy-start.2
  0.7 63.1 %encode_and_route.1 = (bf16[40,4,2,512,128]{4,3,2,1,0:T(8,128)(2,1)}, s32[64]{0:T(128)}) custom-call(s32[2,512]{1,0:T(2,128)} %bitcast.22, s32[512]{0:T(512)} %bitcast.23, s32[512]{0:T(512)} %bitcast.24, bf16[512,512]{1,0:T(8,128)(2,1)} %bitcast.20, bf16[512,128]{1,0:T(8,128)(2,1)} %bitcast.21, bf16[16,512,512]{2,1,0:T(8,128)(2,1)} %bitcast.19), custom_call_target="tpu_custom_call" | custom-call | tf_op jit(solution)/shard_map/encode_and_route/pallas_call | solution.py:551
  63.7 0.0 copy-done
  63.8 0.0 copy-done.1
  63.8 0.0 copy-done.2
  63.8 0.0 copy-start.3
  63.8 0.7 copy-done.3
  64.4 18.2 %decode_and_sketch.1 = (bf16[8,512,512]{2,1,0:T(8,128)(2,1)}, bf16[32,512,128]{2,1,0:T(8,128)(2,1)S(1)}) custom-call(s32[64]{0:T(128)S(1)} %copy-done.3, s32[2,8]{1,0:T(2,128)S(1)} %bitcast.18, bf16[40,4,2,512,128]{4,3,2,1,0:T(8,128)(2,1)} %get-tuple-element.7.shared, bf16[8,512,512]{2,1,0:T(8,128)(2,1)S(1)} %bitcast.15, bf16[32,512,128]{2,1,0:T(8,128)(2,1)S(1)} %bitcast.16), custom_call_target="tpu_custom_call" | custom-call | tf_op jit(solution)/shard_map/decode_and_sketch/pallas_call | solution.py:582
  82.7 26.7 %reduce_sketch.1 = f32[128,128]{1,0:T(8,128)S(1)} custom-call(bf16[4,4,4,2,128,128]{5,4,3,2,1,0:T(8,128)(2,1)S(1)} %bitcast.17), custom_call_target="tpu_custom_call" | custom-call | tf_op jit(solution)/shard_map/reduce_sketch/pallas_call | solution.py:617
  109.4 0.6 copy.12
Async XLA Ops:
  0.6 63.1 %copy-start = (bf16[1,8,512,512]{3,2,1,0:T(8,128)(2,1)S(1)}, bf16[1,8,512,512]{3,2,1,0:T(8,128)(2,1)}, u32[]{:S(2)}) copy-start(bf16[1,8,512,512]{3,2,1,0:T(8,128)(2,1)} %param.15) | copy-start | bytes 12582916
  0.6 63.1 %copy-start.1 = (bf16[16384,128]{1,0:T(8,128)(2,1)S(1)}, bf16[16384,128]{1,0:T(8,128)(2,1)}, u32[]{:S(2)}) copy-start(bf16[16384,128]{1,0:T(8,128)(2,1)} %param.17) | copy-start | bytes 12582916
  0.7 63.1 %copy-start.2 = (s32[1,8,2]{1,2,0:T(2,128)S(1)}, s32[1,8,2]{1,2,0:T(2,128)}, u32[]{:S(2)}) copy-start(s32[1,8,2]{1,2,0:T(2,128)} %param.16) | copy-start | bytes 196
  63.8 0.7 copy-start.3
